TPU v7x, 32 devices: a whole 2x2x4 slice. The times are simulated.
32 devices in a mesh: src: 16 (over z, x, core), tgt: 2 (over y).
Axes of the slice: x: 2, y: 2, z: 4, core: 2. Of those that a mesh axis runs over, the one named last changes fastest.
Arguments:
- source: bfloat16 [8192, 1024], P('src', 'tgt'), may hold values from 0 to 32, as said below
- target: bfloat16 [4096, 1024], P(('tgt', 'src')), may hold values from 0 to 32, as said below
Outputs:
- fwd_mean: float32 [8192], P('src')
- bwd_mean: float32 [4096], P('tgt')
- best_margin: float32 [4, 8192], P(None, 'src')
Inputs may be any that keep to these rules, and one draw needn't show every extreme that they name: `source`: every row has a positive entry. `target`: every row has a positive entry.
All inputs are finite; a program needn't handle non-finite values.
Results may differ from a plain program's by a relative error of at most 0.0003.
Values may be sent and summed in bfloat16 or wider, within the bound.
No kernel may reach another device: no remote copies, remote signals or barrier semaphores. Data moves between devices by JAX's collectives and lax.ppermute only.
A program may use at most 64 MiB of HBM per device.

v0:
```python
import functools
import math

import jax
import jax.numpy as jnp
from jax import lax
from jax.experimental import pallas as pl
from jax.experimental.pallas import tpu as pltpu
from jax.sharding import PartitionSpec as P

K = 4
LANES = 128
SUBLANES = 8


def bits_below(size):
    return [1 << bit for bit in range(size.bit_length() - 1)]


def exchange(values, upper, lower):
    high = jnp.maximum(values[upper], values[lower])
    values[lower] = jnp.minimum(values[upper], values[lower])
    values[upper] = high


def sort_list(values):
    values = list(values)
    for upper, lower in ((0, 1), (2, 3), (0, 2), (1, 3), (1, 2)):
        exchange(values, upper, lower)
    return values


def merge_lists(one, other):
    values = [jnp.maximum(one[k], other[K - 1 - k]) for k in range(K)]
    for upper, lower in ((0, 2), (1, 3), (0, 1), (2, 3)):
        exchange(values, upper, lower)
    return values


def reduce_lists(lists):
    while len(lists) > 1:
        merged = [merge_lists(lists[n], lists[n + 1]) for n in range(0, len(lists) - 1, 2)]
        lists = merged + lists[len(lists) - len(lists) % 2 :]
    return lists[0]


def fold(tile):
    parts = [tile[r : r + SUBLANES] for r in range(0, tile.shape[0], SUBLANES)]
    return reduce_lists([sort_list(parts[n : n + K]) for n in range(0, len(parts), K)])


def fold_sublanes(values):
    shift = SUBLANES // 2
    while shift:
        values = merge_lists(values, [pltpu.roll(v, shift, 0) for v in values])
        shift //= 2
    return values


def store_lists(ref, values, first):
    for k in range(K):
        for n in range(values[k].shape[1] // LANES):
            ref[k, first + n : first + n + 1, :] = values[k][0:1, n * LANES : (n + 1) * LANES]


def inverse_norms(rows):
    width = rows.shape[1]
    values = rows.astype(jnp.float32)
    total = jnp.sum(values * values, axis=1, keepdims=True)
    inverse = lax.rsqrt(total / width + 1e-06) / math.sqrt(width)
    return jnp.broadcast_to(inverse, (rows.shape[0], LANES))


def turn(tile):
    return jnp.concatenate(
        [tile[r : r + LANES].T for r in range(0, tile.shape[0], LANES)], axis=1
    )


def features(ref, groups, rows=slice(None)):
    mine = lax.axis_index("tgt")
    size = ref.shape[1] // groups
    places = [pl.ds(pl.multiple_of((mine ^ t) * size, LANES), size) for t in range(groups)]
    return jnp.concatenate([ref[rows, place] for place in places], axis=1)


def source_rows(piece, first, count):
    columns = []
    for parts in piece:
        at, found = 0, []
        for part in parts:
            low, high = max(first, at), min(first + count, at + part.shape[0])
            if low < high:
                found.append(part[low - at : high - at, :])
            at += part.shape[0]
        columns.append(jnp.concatenate(found, axis=0))
    return jnp.concatenate(columns, axis=1)


def cosine_block(pieces, targets, inv_src, inv_tgt, cos_ref, rows, cols, work):
    groups = len(pieces[0])
    lhs = jnp.concatenate([features(ref, groups) for ref in targets], axis=0)
    n_tgt = lhs.shape[0]
    step = 2 * LANES
    first = 0
    for piece in pieces:
        n_rows = sum(part.shape[0] for part in piece[0])
        for n in range(0, n_rows, step):
            rhs = source_rows(piece, n, step)
            if inv_src[0] is None:
                inverse = turn(inverse_norms(rhs))[0:SUBLANES]
                inv_src[1][:, n : n + step] = inverse
            work[:, first : first + step] = lax.dot_general(
                lhs, rhs, (((1,), (1,)), ((), ())), preferred_element_type=jnp.float32
            )
            first += step
    if inv_tgt[0] is None:
        inv_tgt[1][...] = inverse_norms(lhs)
    inv_t = inv_tgt[0] if inv_tgt[0] is not None else inv_tgt[1]
    col_lists = [[] for _ in range(0, n_tgt, LANES)]
    first = 0
    for b, piece in enumerate(pieces):
        n_rows = sum(part.shape[0] for part in piece[0])
        inv_s = inv_src[0][b] if inv_src[0] is not None else inv_src[1]
        for n in range(0, n_rows, LANES):
            scale = jnp.broadcast_to(inv_s[0:1, n : n + LANES], (LANES, LANES))
            row_lists = []
            if rows[0] is not None:
                row_lists.append([rows[0][b][k, :, n : n + LANES] for k in range(K)])
            for t in range(0, n_tgt, LANES):
                tile = work[t : t + LANES, first : first + LANES] * scale * inv_t[t : t + LANES]
                cos_ref[t : t + LANES, first : first + LANES] = tile
                row_lists.append(fold(tile))
                col_lists[t // LANES].append(fold(tile.T))
            rows[1](b, n, reduce_lists(row_lists))
            first += LANES
    for line, lists in enumerate(col_lists):
        if cols[0] is not None:
            place = slice(line * LANES, (line + 1) * LANES)
            lists.append([cols[0][k, :, place] for k in range(K)])
        cols[1](line, reduce_lists(lists))


def store_running(ref):
    def store(*at):
        *place, values = at
        first = place[-1] if len(place) > 1 else place[0] * LANES
        for k in range(K):
            ref[k, :, first : first + LANES] = values[k]

    return store


def first_kernel(piece, targets, cos_out, inv_src, inv_tgt, rows, cols, work, cos_ref, sem):
    cosine_block(
        [piece], targets, (None, inv_src), (None, inv_tgt), cos_ref,
        (None, store_running(rows)), (None, store_running(cols)), work,
    )
    pltpu.make_async_copy(cos_ref, cos_out, sem).start()
    pltpu.make_async_copy(cos_ref, cos_out, sem).wait()


def next_kernel(piece, targets, inv_tgt, cols_in, cos_ref, inv_src, rows, cols, work):
    cosine_block(
        [piece], targets, (None, inv_src), (inv_tgt, None), cos_ref,
        (None, store_running(rows)), (cols_in, store_running(cols)), work,
    )


def last_kernel(pieces, targets, inv_src, rows_in, cols_in, cos_ref, row_ref, col_ref, work, inv_tgt):
    lines = cols_in.shape[2] // LANES
    slot = rows_in[0].shape[2] // LANES

    def store_row(b, n, values):
        store_lists(row_ref, fold_sublanes(values), b * slot + n // LANES)

    def store_col(line, values):
        store_lists(col_ref, fold_sublanes(values), lines + line)

    cosine_block(
        pieces, targets, (inv_src, None), (None, inv_tgt), cos_ref,
        (rows_in, store_row), (None, store_col), work,
    )
    for line in range(lines):
        place = slice(line * LANES, (line + 1) * LANES)
        store_lists(col_ref, fold_sublanes([cols_in[k, :, place] for k in range(K)]), line)


def flipped(ref, k, unit):
    if unit >= LANES:
        step = unit // LANES
        firsts = [line ^ step for line in range(0, ref.shape[1], step)]
        return jnp.concatenate([ref[k, first : first + step, :] for first in firsts], axis=0)
    values = ref[k]
    if unit:
        lane = lax.broadcasted_iota(jnp.int32, values.shape, 1)
        up, down = pltpu.roll(values, LANES - unit, 1), pltpu.roll(values, unit, 1)
        values = jnp.where((lane & unit) == 0, up, down)
    return values


def merged(mine, arrived, unit):
    return merge_lists([mine[k] for k in range(K)], [flipped(arrived, k, unit) for k in range(K)])


def merge_kernel(unit, mine, arrived, out_ref):
    for k, values in enumerate(merged(mine, arrived, unit)):
        out_ref[k] = values


def spread(ref, line):
    return jnp.broadcast_to(ref[line : line + 1, :] * 0.5, (LANES, LANES))


def margin_kernel(unit, first, early, late, rows, cols, out_ref, fwd_ref, bwd_ref, bwd_down, held, sem):
    n_early, slot = first.shape
    n_late, n_src = late.shape
    arriving = pltpu.make_async_copy(first, held, sem)
    arriving.start()
    early = [held, *early]
    fwd_ref[...] = sum(merged(*rows, 0)) / K
    bwd_ref[...] = sum(merged(*cols, unit)) / K
    for t in range(0, n_early + n_late, LANES):
        bwd_down[t : t + LANES, :] = spread(bwd_ref, t // LANES).T
    for s in [*range(slot, n_src, LANES), *range(0, slot, LANES)]:
        if s == 0:
            arriving.wait()
        fwd = spread(fwd_ref, s // LANES)
        lists = []
        for t in range(0, n_early + n_late, LANES):
            if t < n_early:
                tile = early[s // slot][t : t + LANES, s % slot : s % slot + LANES]
            else:
                tile = late[t - n_early : t - n_early + LANES, s : s + LANES]
            lists.append(fold(tile / (fwd + bwd_down[t : t + LANES, :])))
        store_lists(out_ref, fold_sublanes(reduce_lists(lists)), s // LANES)


def place_kernel(near, far, lines, known, out_ref):
    at = lax.axis_index("src")
    for b in range(near):
        for a in range(far):
            for c in range(2):
                slot = (b * far + a) * 2 + c
                first = (at ^ ((a * near + b) * 2 + c)) * lines
                out_ref[pl.ds(first, lines), :] = known[slot * lines : (slot + 1) * lines, :]


def prepare_kernel(source, target, source_out, target_out, sems):
    copies = [
        pltpu.make_async_copy(source, source_out, sems.at[0]),
        pltpu.make_async_copy(target, target_out, sems.at[1]),
    ]
    for copy in copies:
        copy.start()
    for copy in copies:
        copy.wait()


def call(kernel, args, out_shapes, scratch=(), flops=0, hbm_in=(), hbm_out=(), sems=0):
    vmem = pl.BlockSpec(memory_space=pltpu.VMEM)
    hbm = pl.BlockSpec(memory_space=pltpu.HBM)
    in_specs = [
        jax.tree.map(lambda _: hbm if n in hbm_in else vmem, arg) for n, arg in enumerate(args)
    ]
    return pl.pallas_call(
        kernel,
        out_shape=tuple(jax.ShapeDtypeStruct(shape, jnp.float32) for shape in out_shapes),
        in_specs=in_specs,
        out_specs=tuple(hbm if n in hbm_out else vmem for n in range(len(out_shapes))),
        scratch_shapes=[pltpu.VMEM(shape, jnp.float32) for shape in scratch]
        + [pltpu.SemaphoreType.DMA] * sems,
        compiler_params=pltpu.CompilerParams(vmem_limit_bytes=16 << 20),
        cost_estimate=pl.CostEstimate(flops=flops, transcendentals=0, bytes_accessed=0),
    )(*args)


def merge_arrays(one, other, unit=0):
    return call(functools.partial(merge_kernel, unit), (one, other), [one.shape])[0]


def prepare(source, target):
    return pl.pallas_call(
        prepare_kernel,
        out_shape=tuple(jax.ShapeDtypeStruct(a.shape, a.dtype) for a in (source, target)),
        in_specs=[pl.BlockSpec(memory_space=pl.ANY)] * 2,
        out_specs=(pl.BlockSpec(memory_space=pltpu.VMEM),) * 2,
        scratch_shapes=[pltpu.SemaphoreType.DMA((2,))],
        compiler_params=pltpu.CompilerParams(vmem_limit_bytes=4 << 20),
        name="prepare",
    )(source, target)


def xor_pairs(size, mask):
    return [(i, i ^ mask) for i in range(size)]


def flip(array, axis, mask):
    shape = array.shape
    split = shape[:axis] + (shape[axis] // (2 * mask), 2, mask) + shape[axis + 1 :]
    parts = array.reshape(split)
    low = lax.slice_in_dim(parts, 0, 1, axis=axis + 1)
    high = lax.slice_in_dim(parts, 1, 2, axis=axis + 1)
    return jnp.concatenate([high, low], axis=axis + 1).reshape(shape)


def flip_where(bit, array, axis, mask):
    return jnp.where(bit != 0, flip(array, axis, mask), array)


def solution(mesh):
    n_src, n_tgt = mesh.shape["src"], mesh.shape["tgt"]
    near = 1 << (((n_src // 2).bit_length() - 1) // 2)
    far = n_src // 2 // near

    def over_src(array, mask):
        return lax.ppermute(array, "src", xor_pairs(n_src, mask))

    def over_tgt(array, mask):
        return lax.ppermute(array, "tgt", xor_pairs(n_tgt, mask))

    def over_both(array, src_mask, tgt_mask):
        pairs = xor_pairs(n_src * n_tgt, src_mask * n_tgt + tgt_mask)
        return lax.ppermute(array, ("src", "tgt"), pairs)

    def local(source, target):
        rows, _ = source.shape
        t_rows, width = target.shape
        own_source, own_target = prepare(source, target)
        pieces = [[None] * n_tgt for _ in range(near)]
        square = (near, n_tgt) == (2, 2)
        held = [own_target] + [None] * (far - 1)
        for t in range(n_tgt):
            for b in range(near):
                if (b, t) == (0, 0):
                    pieces[b][t] = [own_source]
                elif not (square and b and t):
                    pieces[b][t] = [over_both(source, 2 * b, t)]
        for a in range(1, far):
            if (far, a) != (4, 3):
                held[a] = over_src(target, 2 * near * a)
        if square:
            half = rows // 2
            low = over_src(pieces[0][1][0][:half], 2)
            high = over_tgt(pieces[1][0][0][half:], 1)
            pieces[1][1] = [low, high]
        if far == 4:
            held[3] = over_src(held[2], 2 * near)
        pairs = []
        for a in range(far):
            pairs.append([held[a], over_src(held[a] if a else target, 1)])
        n_late = max(1, LANES // (2 * t_rows))
        early = sum(pairs[: far - n_late], [])
        late = sum(pairs[far - n_late :], [])
        e_rows, l_rows = len(early) * t_rows, len(late) * t_rows
        block_src, block_tgt = near * rows, 2 * far * t_rows
        src_lines, tgt_lines = block_src // LANES, block_tgt // LANES
        running = (K, SUBLANES, rows), (K, SUBLANES, e_rows)
        cos, inv, inv_tgt, row_run, cols = call(
            first_kernel, (pieces[0], early),
            [(e_rows, rows), (SUBLANES, rows), (e_rows, LANES), *running],
            [(e_rows, rows)] * 2, 2 * e_rows * rows * width, hbm_out=(0,), sems=1,
        )
        cosines, inverses, row_runs = [cos], [inv], [row_run]
        for b in range(1, near):
            cos, inv, row_run, cols = call(
                next_kernel, (pieces[b], early, inv_tgt, cols),
                [(e_rows, rows), (SUBLANES, rows), *running],
                [(e_rows, rows)], 2 * e_rows * rows * width,
            )
            cosines.append(cos)
            inverses.append(inv)
            row_runs.append(row_run)
        cos_late, row_best, col_best = call(
            last_kernel, (pieces, late, inverses, row_runs, cols),
            [(l_rows, block_src), (K, src_lines, LANES), (K, tgt_lines, LANES)],
            [(l_rows, block_src), (l_rows, LANES)], 2 * l_rows * block_src * width,
        )

        col_best = merge_arrays(col_best, over_src(col_best, 1), t_rows)
        for bit in bits_below(near):
            row_best = merge_arrays(row_best, over_src(row_best, 2 * bit), bit * rows)
        for bit in bits_below(far)[:-1]:
            col_best = merge_arrays(col_best, over_src(col_best, 2 * near * bit), 2 * bit * t_rows)
        for bit in bits_below(n_tgt)[:-1]:
            row_best = merge_arrays(row_best, over_tgt(row_best, bit))
        row_pair = [row_best, over_tgt(row_best, n_tgt // 2)]
        col_pair = [col_best, over_src(col_best, near * far)]
        margins, fwd, bwd = call(
            functools.partial(margin_kernel, far * t_rows),
            (cosines[0], cosines[1:], cos_late, row_pair, col_pair),
            [(K, src_lines, LANES), (src_lines, LANES), (tgt_lines, LANES)],
            [(block_tgt, LANES), cosines[0].shape], hbm_in=(0,), sems=1,
        )
        best = margins.reshape(K, near, rows // LANES, LANES)
        known = bwd.reshape(1, tgt_lines, LANES)
        kept = list(range(near))
        for bit in bits_below(near):
            send = [n for n, slot in enumerate(kept) if slot & bit]
            keep = [n for n, slot in enumerate(kept) if not slot & bit]
            lists = jnp.concatenate([best[:, n : n + 1] for n in send], axis=1)
            split = lists.size // LANES
            payload = jnp.concatenate(
                [lists.reshape(split, LANES), known.reshape(-1, LANES)], axis=0
            )
            arrived = over_src(payload, 2 * bit)
            mine = jnp.concatenate([best[:, n : n + 1] for n in keep], axis=1)
            arrived_lists = arrived[:split].reshape(K, -1, LANES)
            best = merge_arrays(mine.reshape(arrived_lists.shape), arrived_lists).reshape(mine.shape)
            known = jnp.concatenate([known, arrived[split:].reshape(known.shape)], axis=0)
            kept = [kept[n] for n in keep]
        best = best.reshape(K, rows // LANES, LANES)
        for bit in bits_below(n_tgt):
            best = merge_arrays(best, over_tgt(best, bit))
        if t_rows % LANES == 0:
            lines = t_rows // LANES
            (bwd_mean,) = call(
                functools.partial(place_kernel, near, far, lines),
                (known.reshape(-1, LANES),), [(near * tgt_lines, LANES)],
            )
            return fwd[: rows // LANES].reshape(-1), bwd_mean.reshape(-1), best.reshape(K, rows)
        at = lax.axis_index("src")
        known = known.reshape(near, far, 2, t_rows)
        for axis, size, unit in ((0, near, 2), (1, far, 2 * near), (2, 2, 1)):
            for bit in bits_below(size):
                known = flip_where(at & (unit * bit), known, axis, bit)
        bwd_mean = known.transpose(1, 0, 2, 3).reshape(-1)
        return fwd[: rows // LANES].reshape(-1), bwd_mean, best.reshape(K, rows)

    in_specs = (P("src", "tgt"), P(("tgt", "src"), None))
    out_specs = (P("src"), P("tgt"), P(None, "src"))

    return jax.shard_map(local, mesh=mesh, in_specs=in_specs, out_specs=out_specs, check_vma=False)
```

profile of v0, /device:TPU:0, one launch (start us, length us, event | category | flops | bytes accessed | tf_op | source)
XLA Modules:
  0.0 53.2 jit_solution(14285251562223996607)
XLA Ops:
  0.6 3.1 %collective-permute-start = (bf16[512,512]{1,0:T(8,128)(2,1)}, bf16[512,512]{1,0:T(8,128)(2,1)S(1)}, u32[]{:S(2)}, u32[]{:S(2)}) collective-permute-start(bf16[512,512]{1,0:T(8,128)(2,1)} %source.1), channel_id=1, source_target_pairs={{0,1},{1,0},{2,3},{3,2},{4,5},{5,4},{6,7},{7,6},{8,9},{9,8},{10,11... | collective-permute-start | bytes 1572872 | tf_op jit(solution)/shard_map/ppermute | solution.py:324
  3.7 1.5 %collective-permute-start.6 = (bf16[512,512]{1,0:T(8,128)(2,1)}, bf16[512,512]{1,0:T(8,128)(2,1)S(1)}, u32[]{:S(2)}, u32[]{:S(2)}) collective-permute-start(bf16[512,512]{1,0:T(8,128)(2,1)} %source.1), channel_id=1, source_target_pairs={{0,4},{1,5},{2,6},{3,7},{4,0},{5,1},{6,2},{7,3},{8,12},{9,13},{10,... | collective-permute-start | bytes 1572872 | tf_op jit(solution)/shard_map/ppermute | solution.py:324
  5.2 2.6 %collective-permute-start.4 = (bf16[128,1024]{1,0:T(8,128)(2,1)}, bf16[128,1024]{1,0:T(8,128)(2,1)S(1)}, u32[]{:S(2)}, u32[]{:S(2)}) collective-permute-start(bf16[128,1024]{1,0:T(8,128)(2,1)} %target.1), channel_id=1, source_target_pairs={{0,16},{2,18},{4,20},{6,22},{8,24},{10,26},{12,28},{14,30},{16,0},... | collective-permute-start | bytes 786440 | tf_op jit(solution)/shard_map/ppermute | solution.py:317
  7.8 1.6 %collective-permute-start.2 = (bf16[128,1024]{1,0:T(8,128)(2,1)}, bf16[128,1024]{1,0:T(8,128)(2,1)S(1)}, u32[]{:S(2)}, u32[]{:S(2)}) collective-permute-start(bf16[128,1024]{1,0:T(8,128)(2,1)} %target.1), channel_id=1, source_target_pairs={{0,8},{2,10},{4,12},{6,14},{8,0},{10,2},{12,4},{14,6},{16,24},{18,... | collective-permute-start | bytes 786440 | tf_op jit(solution)/shard_map/ppermute | solution.py:317
  9.4 10.1 %collective-permute-done.4.targets_4_ = bf16[128,1024]{1,0:T(8,128)(2,1)S(1)} collective-permute-done((bf16[128,1024]{1,0:T(8,128)(2,1)}, bf16[128,1024]{1,0:T(8,128)(2,1)S(1)}, u32[]{:S(2)}, u32[]{:S(2)}) %collective-permute-start.4) | collective-permute-done | bytes 262176 | tf_op jit(solution)/shard_map/ppermute | solution.py:317
  19.5 0.7 %collective-permute-start.9 = (bf16[128,1024]{1,0:T(8,128)(2,1)S(1)}, bf16[128,1024]{1,0:T(8,128)(2,1)S(1)}, u32[]{:S(2)}, u32[]{:S(2)}) collective-permute-start(bf16[128,1024]{1,0:T(8,128)(2,1)S(1)} %collective-permute-done.4.targets_4_), channel_id=1, source_target_pairs={{0,8},{2,10},{4,12},{6,14},{8,0},{10,2},{12,4},{14,6},{16,24},{18,... | collective-permute-start | bytes 786440 | tf_op jit(solution)/shard_map/ppermute | solution.py:317
  20.2 0.5 collective-permute-start.3
  20.7 0.6 %collective-permute-start.7 = (bf16[256,512]{1,0:T(8,128)(2,1)S(1)}, bf16[256,512]{1,0:T(8,128)(2,1)S(1)}, u32[]{:S(2)}, u32[]{:S(2)}) collective-permute-start(bf16[256,512]{1,0:T(8,128)(2,1)S(1)} %slice.28), channel_id=1, source_target_pairs={{0,4},{2,6},{4,0},{6,2},{8,12},{10,14},{12,8},{14,10},{16,20},{18,... | collective-permute-start | bytes 786440 | tf_op jit(solution)/shard_map/ppermute | solution.py:317
  21.4 0.6 %collective-permute-start.8 = (bf16[256,512]{1,0:T(8,128)(2,1)S(1)}, bf16[256,512]{1,0:T(8,128)(2,1)S(1)}, u32[]{:S(2)}, u32[]{:S(2)}) collective-permute-start(bf16[256,512]{1,0:T(8,128)(2,1)S(1)} %slice.29), channel_id=1, source_target_pairs={{0,1},{1,0},{2,3},{3,2},{4,5},{5,4},{6,7},{7,6},{8,9},{9,8},{10,11... | collective-permute-start | bytes 786440 | tf_op jit(solution)/shard_map/ppermute | solution.py:320
  21.9 4.7 %collective-permute-done.9.targets_0_ = bf16[128,1024]{1,0:T(8,128)(2,1)S(1)} collective-permute-done((bf16[128,1024]{1,0:T(8,128)(2,1)S(1)}, bf16[128,1024]{1,0:T(8,128)(2,1)S(1)}, u32[]{:S(2)}, u32[]{:S(2)}) %collective-permute-start.9) | collective-permute-done | bytes 262176 | tf_op jit(solution)/shard_map/ppermute | solution.py:317
  26.7 1.0 %copy-done = bf16[512,512]{1,0:T(8,128)(2,1)S(1)} copy-done((bf16[512,512]{1,0:T(8,128)(2,1)S(1)}, bf16[512,512]{1,0:T(8,128)(2,1)}, u32[]{:S(2)}) %copy-start) | copy-done | bytes 524312
  27.7 0.9 %copy-done.1 = bf16[128,1024]{1,0:T(8,128)(2,1)S(1)} copy-done((bf16[128,1024]{1,0:T(8,128)(2,1)S(1)}, bf16[128,1024]{1,0:T(8,128)(2,1)}, u32[]{:S(2)}) %copy-start.1) | copy-done | bytes 262168
  28.8 1.8 %shard_map.49 = (f32[768,512]{1,0:T(8,128)S(1)}, f32[8,512]{1,0:T(8,128)S(1)}, f32[768,128]{1,0:T(8,128)S(1)}, f32[4,8,512]{2,1,0:T(8,128)S(1)}, f32[4,8,768]{2,1,0:T(8,128)S(1)}) custom-call(bf16[512,512]{1,0:T(8,128)(2,1)S(1)} %get-tuple-element.20.piece_0__0_.pieces_0__0__0_, bf16[512,512]{1,0:T(8,128)(2,1)S(1)} %collective-permute-done.piece_1__0_.pieces_0__1__0_, ...), custom_call_target="tpu_custom_call" | custom-call | flops 805306368 | tf_op jit(solution)/shard_map/pallas_call | solution.py:266
  30.5 1.6 %shard_map.50 = (f32[768,512]{1,0:T(8,128)S(1)}, f32[8,512]{1,0:T(8,128)S(1)}, f32[4,8,512]{2,1,0:T(8,128)S(1)}, f32[4,8,768]{2,1,0:T(8,128)S(1)}) custom-call(bf16[512,512]{1,0:T(8,128)(2,1)S(1)} %collective-permute-done.6.piece_0__0_.pieces_1__0__0_, bf16[256,512]{1,0:T(8,128)(2,1)S(1)} %collective-permute-done.7.piece_1__0_.pieces_1__1__0_, ...), custom_call_target="tpu_custom_call" | custom-call | flops 805306368 | tf_op jit(solution)/shard_map/pallas_call | solution.py:266
  32.2 1.1 %shard_map.51 = (f32[256,1024]{1,0:T(8,128)S(1)}, f32[4,8,128]{2,1,0:T(8,128)S(1)}, f32[4,8,128]{2,1,0:T(8,128)S(1)}) custom-call(bf16[512,512]{1,0:T(8,128)(2,1)S(1)} %get-tuple-element.20.piece_0__0_.pieces_0__0__0_, bf16[512,512]{1,0:T(8,128)(2,1)S(1)} %collective-permute-done.piece_1__0_.pieces_0__1__0_, ...), custom_call_target="tpu_custom_call" | custom-call | flops 536870912 | tf_op jit(solution)/shard_map/pallas_call | solution.py:266
  33.3 0.6 %collective-permute-start.13 = (f32[4,8,128]{2,1,0:T(8,128)S(1)}, f32[4,8,128]{2,1,0:T(8,128)S(1)}, u32[]{:S(2)}, u32[]{:S(2)}) collective-permute-start(f32[4,8,128]{2,1,0:T(8,128)S(1)} %get-tuple-element.33.mine), channel_id=1, source_target_pairs={{0,2},{2,0},{4,6},{6,4},{8,10},{10,8},{12,14},{14,12},{16,18},{18,... | collective-permute-start | bytes 49160 | tf_op jit(solution)/shard_map/ppermute | solution.py:317
  33.9 0.5 %collective-permute-start.11 = (f32[4,8,128]{2,1,0:T(8,128)S(1)}, f32[4,8,128]{2,1,0:T(8,128)S(1)}, u32[]{:S(2)}, u32[]{:S(2)}) collective-permute-start(f32[4,8,128]{2,1,0:T(8,128)S(1)} %get-tuple-element.32.mine), channel_id=1, source_target_pairs={{0,4},{2,6},{4,0},{6,2},{8,12},{10,14},{12,8},{14,10},{16,20},{18,... | collective-permute-start | bytes 49160 | tf_op jit(solution)/shard_map/ppermute | solution.py:317
  34.4 0.3 collective-permute-done.13.arrived
  34.7 1.8 %collective-permute-start.14 = (f32[4,8,128]{2,1,0:T(8,128)S(1)}, f32[4,8,128]{2,1,0:T(8,128)S(1)}, u32[]{:S(2)}, u32[]{:S(2)}) collective-permute-start(f32[4,8,128]{2,1,0:T(8,128)S(1)} %shard_map.53.mine), channel_id=1, source_target_pairs={{0,8},{2,10},{4,12},{6,14},{8,0},{10,2},{12,4},{14,6},{16,24},{18,... | collective-permute-start | bytes 49160 | tf_op jit(solution)/shard_map/ppermute | solution.py:317
  36.5 1.1 %collective-permute-done.11.arrived = f32[4,8,128]{2,1,0:T(8,128)S(1)} collective-permute-done((f32[4,8,128]{2,1,0:T(8,128)S(1)}, f32[4,8,128]{2,1,0:T(8,128)S(1)}, u32[]{:S(2)}, u32[]{:S(2)}) %collective-permute-start.11) | collective-permute-done | bytes 16416 | tf_op jit(solution)/shard_map/ppermute | solution.py:317
  37.6 0.6 %collective-permute-start.12 = (f32[4,8,128]{2,1,0:T(8,128)S(1)}, f32[4,8,128]{2,1,0:T(8,128)S(1)}, u32[]{:S(2)}, u32[]{:S(2)}) collective-permute-start(f32[4,8,128]{2,1,0:T(8,128)S(1)} %shard_map.52.rows_0_), channel_id=1, source_target_pairs={{0,1},{1,0},{2,3},{3,2},{4,5},{5,4},{6,7},{7,6},{8,9},{9,8},{10,11... | collective-permute-start | bytes 49160 | tf_op jit(solution)/shard_map/ppermute | solution.py:320
  38.2 0.4 collective-permute-done.14.arrived
  38.5 3.3 %collective-permute-start.15 = (f32[4,8,128]{2,1,0:T(8,128)S(1)}, f32[4,8,128]{2,1,0:T(8,128)S(1)}, u32[]{:S(2)}, u32[]{:S(2)}) collective-permute-start(f32[4,8,128]{2,1,0:T(8,128)S(1)} %shard_map.54.cols_0_), channel_id=1, source_target_pairs={{0,16},{2,18},{4,20},{6,22},{8,24},{10,26},{12,28},{14,30},{16,0},... | collective-permute-start | bytes 49160 | tf_op jit(solution)/shard_map/ppermute | solution.py:317
  41.9 1.7 %collective-permute-done.15.cols_1_ = f32[4,8,128]{2,1,0:T(8,128)S(1)} collective-permute-done((f32[4,8,128]{2,1,0:T(8,128)S(1)}, f32[4,8,128]{2,1,0:T(8,128)S(1)}, u32[]{:S(2)}, u32[]{:S(2)}) %collective-permute-start.15) | collective-permute-done | bytes 16416 | tf_op jit(solution)/shard_map/ppermute | solution.py:317
  43.6 1.5 %shard_map.55 = (f32[4,8,128]{2,1,0:T(8,128)S(1)}, f32[8,128]{1,0:T(8,128)S(1)}, f32[8,128]{1,0:T(8,128)S(1)}) custom-call(f32[768,512]{1,0:T(8,128)S(1)} %get-tuple-element.22.first, f32[768,512]{1,0:T(8,128)S(1)} %get-tuple-element.25.early_0_, f32[256,1024]{1,0:T(8,128)S(1)} %get-tuple-element.31.late, f32[4,8,128]{2,1,0:T(8,128)S(1)} %shard_map.52.rows_0_, ...), custom_call_target="tpu_custom_call" | custom-call | tf_op jit(solution)/shard_map/pallas_call | solution.py:266
  45.1 1.3 %collective-permute-start.16 = (f32[24,128]{1,0:T(8,128)S(1)}, f32[24,128]{1,0:T(8,128)S(1)}, u32[]{:S(2)}, u32[]{:S(2)}) collective-permute-start(f32[24,128]{1,0:T(8,128)S(1)} %pad_maximum_fusion), channel_id=1, source_target_pairs={{0,4},{2,6},{4,0},{6,2},{8,12},{10,14},{12,8},{14,10},{16,20},{18,... | collective-permute-start | bytes 36872 | tf_op jit(solution)/shard_map/ppermute | solution.py:317
  46.3 0.6 %slice_bitcast_fusion.2 = f32[512]{0:T(512)} fusion(f32[8,128]{1,0:T(8,128)S(1)} %get-tuple-element.34), kind=kLoop, calls=%fused_computation.5 | loop fusion | bytes 4096 | tf_op jit(solution)/shard_map/reshape | solution.py:421
  46.9 1.9 %collective-permute-done.16 = f32[24,128]{1,0:T(8,128)S(1)} collective-permute-done((f32[24,128]{1,0:T(8,128)S(1)}, f32[24,128]{1,0:T(8,128)S(1)}, u32[]{:S(2)}, u32[]{:S(2)}) %collective-permute-start.16) | collective-permute-done | bytes 12320 | tf_op jit(solution)/shard_map/ppermute | solution.py:317
  48.9 1.2 %collective-permute-start.17 = (f32[4,4,128]{2,1,0:T(4,128)S(1)}, f32[4,4,128]{2,1,0:T(4,128)S(1)}, u32[]{:S(2)}, u32[]{:S(2)}) collective-permute-start(f32[4,4,128]{2,1,0:T(4,128)S(1)} %shard_map.57.mine), channel_id=1, source_target_pairs={{0,1},{1,0},{2,3},{3,2},{4,5},{5,4},{6,7},{7,6},{8,9},{9,8},{10,11... | collective-permute-start | bytes 24584 | tf_op jit(solution)/shard_map/ppermute | solution.py:320
  50.1 0.6 %shard_map.56 = f32[16,128]{1,0:T(8,128)} custom-call(f32[16,128]{1,0:T(8,128)S(1)} %maximum_bitcast_fusion.known), custom_call_target="tpu_custom_call" | custom-call | tf_op jit(solution)/shard_map/pallas_call | solution.py:266
  50.7 1.8 %collective-permute-done.17.arrived = f32[4,4,128]{2,1,0:T(4,128)S(1)} collective-permute-done((f32[4,4,128]{2,1,0:T(4,128)S(1)}, f32[4,4,128]{2,1,0:T(4,128)S(1)}, u32[]{:S(2)}, u32[]{:S(2)}) %collective-permute-start.17) | collective-permute-done | bytes 8224 | tf_op jit(solution)/shard_map/ppermute | solution.py:320
  52.6 0.6 %copy.9 = f32[1,4,4,128]{3,1,2,0:T(4,128)} copy(f32[1,4,4,128]{3,2,1,0:T(4,128)S(1)} %bitcast.20) | data formatting | bytes 16384
  (28 shorter events, 0.2 us)
Async XLA Ops:
  0.6 19.6 %collective-permute-start = (bf16[512,512]{1,0:T(8,128)(2,1)}, bf16[512,512]{1,0:T(8,128)(2,1)S(1)}, u32[]{:S(2)}, u32[]{:S(2)}) collective-permute-start(bf16[512,512]{1,0:T(8,128)(2,1)} %source.1), channel_id=1, source_target_pairs={{0,1},{1,0},{2,3},{3,2},{4,5},{5,4},{6,7},{7,6},{8,9},{9,8},{10,11... | collective-permute-start | bytes 1572872 | tf_op jit(solution)/shard_map/ppermute | solution.py:324
  3.7 17.0 %collective-permute-start.6 = (bf16[512,512]{1,0:T(8,128)(2,1)}, bf16[512,512]{1,0:T(8,128)(2,1)S(1)}, u32[]{:S(2)}, u32[]{:S(2)}) collective-permute-start(bf16[512,512]{1,0:T(8,128)(2,1)} %source.1), channel_id=1, source_target_pairs={{0,4},{1,5},{2,6},{3,7},{4,0},{5,1},{6,2},{7,3},{8,12},{9,13},{10,... | collective-permute-start | bytes 1572872 | tf_op jit(solution)/shard_map/ppermute | solution.py:324
  5.2 14.3 %collective-permute-start.4 = (bf16[128,1024]{1,0:T(8,128)(2,1)}, bf16[128,1024]{1,0:T(8,128)(2,1)S(1)}, u32[]{:S(2)}, u32[]{:S(2)}) collective-permute-start(bf16[128,1024]{1,0:T(8,128)(2,1)} %target.1), channel_id=1, source_target_pairs={{0,16},{2,18},{4,20},{6,22},{8,24},{10,26},{12,28},{14,30},{16,0},... | collective-permute-start | bytes 786440 | tf_op jit(solution)/shard_map/ppermute | solution.py:317
  7.8 12.4 %collective-permute-start.2 = (bf16[128,1024]{1,0:T(8,128)(2,1)}, bf16[128,1024]{1,0:T(8,128)(2,1)S(1)}, u32[]{:S(2)}, u32[]{:S(2)}) collective-permute-start(bf16[128,1024]{1,0:T(8,128)(2,1)} %target.1), channel_id=1, source_target_pairs={{0,8},{2,10},{4,12},{6,14},{8,0},{10,2},{12,4},{14,6},{16,24},{18,... | collective-permute-start | bytes 786440 | tf_op jit(solution)/shard_map/ppermute | solution.py:317
  9.3 12.0 %collective-permute-start.1 = (bf16[128,1024]{1,0:T(8,128)(2,1)}, bf16[128,1024]{1,0:T(8,128)(2,1)S(1)}, u32[]{:S(2)}, u32[]{:S(2)}) collective-permute-start(bf16[128,1024]{1,0:T(8,128)(2,1)} %target.1), channel_id=1, source_target_pairs={{0,2},{2,0},{4,6},{6,4},{8,10},{10,8},{12,14},{14,12},{16,18},{18,... | collective-permute-start | bytes 786440 | tf_op jit(solution)/shard_map/ppermute | solution.py:317
  19.5 7.2 %collective-permute-start.9 = (bf16[128,1024]{1,0:T(8,128)(2,1)S(1)}, bf16[128,1024]{1,0:T(8,128)(2,1)S(1)}, u32[]{:S(2)}, u32[]{:S(2)}) collective-permute-start(bf16[128,1024]{1,0:T(8,128)(2,1)S(1)} %collective-permute-done.4.targets_4_), channel_id=1, source_target_pairs={{0,8},{2,10},{4,12},{6,14},{8,0},{10,2},{12,4},{14,6},{16,24},{18,... | collective-permute-start | bytes 786440 | tf_op jit(solution)/shard_map/ppermute | solution.py:317
  20.2 8.6 %collective-permute-start.5 = (bf16[128,1024]{1,0:T(8,128)(2,1)S(1)}, bf16[128,1024]{1,0:T(8,128)(2,1)S(1)}, u32[]{:S(2)}, u32[]{:S(2)}) collective-permute-start(bf16[128,1024]{1,0:T(8,128)(2,1)S(1)} %collective-permute-done.4.targets_4_), channel_id=1, source_target_pairs={{0,2},{2,0},{4,6},{6,4},{8,10},{10,8},{12,14},{14,12},{16,18},{18,... | collective-permute-start | bytes 786440 | tf_op jit(solution)/shard_map/ppermute | solution.py:317
  20.2 8.6 %collective-permute-start.3 = (bf16[128,1024]{1,0:T(8,128)(2,1)S(1)}, bf16[128,1024]{1,0:T(8,128)(2,1)S(1)}, u32[]{:S(2)}, u32[]{:S(2)}) collective-permute-start(bf16[128,1024]{1,0:T(8,128)(2,1)S(1)} %collective-permute-done.2.targets_2_), channel_id=1, source_target_pairs={{0,2},{2,0},{4,6},{6,4},{8,10},{10,8},{12,14},{14,12},{16,18},{18,... | collective-permute-start | bytes 786440 | tf_op jit(solution)/shard_map/ppermute | solution.py:317
  20.7 9.8 %collective-permute-start.7 = (bf16[256,512]{1,0:T(8,128)(2,1)S(1)}, bf16[256,512]{1,0:T(8,128)(2,1)S(1)}, u32[]{:S(2)}, u32[]{:S(2)}) collective-permute-start(bf16[256,512]{1,0:T(8,128)(2,1)S(1)} %slice.28), channel_id=1, source_target_pairs={{0,4},{2,6},{4,0},{6,2},{8,12},{10,14},{12,8},{14,10},{16,20},{18,... | collective-permute-start | bytes 786440 | tf_op jit(solution)/shard_map/ppermute | solution.py:317
  21.4 9.2 %collective-permute-start.8 = (bf16[256,512]{1,0:T(8,128)(2,1)S(1)}, bf16[256,512]{1,0:T(8,128)(2,1)S(1)}, u32[]{:S(2)}, u32[]{:S(2)}) collective-permute-start(bf16[256,512]{1,0:T(8,128)(2,1)S(1)} %slice.29), channel_id=1, source_target_pairs={{0,1},{1,0},{2,3},{3,2},{4,5},{5,4},{6,7},{7,6},{8,9},{9,8},{10,11... | collective-permute-start | bytes 786440 | tf_op jit(solution)/shard_map/ppermute | solution.py:320
  26.7 5.5 %collective-permute-start.10 = (bf16[128,1024]{1,0:T(8,128)(2,1)S(1)}, bf16[128,1024]{1,0:T(8,128)(2,1)S(1)}, u32[]{:S(2)}, u32[]{:S(2)}) collective-permute-start(bf16[128,1024]{1,0:T(8,128)(2,1)S(1)} %collective-permute-done.9.targets_0_), channel_id=1, source_target_pairs={{0,2},{2,0},{4,6},{6,4},{8,10},{10,8},{12,14},{14,12},{16,18},{18,... | collective-permute-start | bytes 786440 | tf_op jit(solution)/shard_map/ppermute | solution.py:317
  26.7 1.0 %copy-start = (bf16[512,512]{1,0:T(8,128)(2,1)S(1)}, bf16[512,512]{1,0:T(8,128)(2,1)}, u32[]{:S(2)}) copy-start(bf16[512,512]{1,0:T(8,128)(2,1)} %source.1) | copy-start | bytes 1572868
  27.7 0.9 %copy-start.1 = (bf16[128,1024]{1,0:T(8,128)(2,1)S(1)}, bf16[128,1024]{1,0:T(8,128)(2,1)}, u32[]{:S(2)}) copy-start(bf16[128,1024]{1,0:T(8,128)(2,1)} %target.1) | copy-start | bytes 786436
  33.3 1.4 %collective-permute-start.13 = (f32[4,8,128]{2,1,0:T(8,128)S(1)}, f32[4,8,128]{2,1,0:T(8,128)S(1)}, u32[]{:S(2)}, u32[]{:S(2)}) collective-permute-start(f32[4,8,128]{2,1,0:T(8,128)S(1)} %get-tuple-element.33.mine), channel_id=1, source_target_pairs={{0,2},{2,0},{4,6},{6,4},{8,10},{10,8},{12,14},{14,12},{16,18},{18,... | collective-permute-start | bytes 49160 | tf_op jit(solution)/shard_map/ppermute | solution.py:317
  33.9 3.7 %collective-permute-start.11 = (f32[4,8,128]{2,1,0:T(8,128)S(1)}, f32[4,8,128]{2,1,0:T(8,128)S(1)}, u32[]{:S(2)}, u32[]{:S(2)}) collective-permute-start(f32[4,8,128]{2,1,0:T(8,128)S(1)} %get-tuple-element.32.mine), channel_id=1, source_target_pairs={{0,4},{2,6},{4,0},{6,2},{8,12},{10,14},{12,8},{14,10},{16,20},{18,... | collective-permute-start | bytes 49160 | tf_op jit(solution)/shard_map/ppermute | solution.py:317
  34.7 3.8 %collective-permute-start.14 = (f32[4,8,128]{2,1,0:T(8,128)S(1)}, f32[4,8,128]{2,1,0:T(8,128)S(1)}, u32[]{:S(2)}, u32[]{:S(2)}) collective-permute-start(f32[4,8,128]{2,1,0:T(8,128)S(1)} %shard_map.53.mine), channel_id=1, source_target_pairs={{0,8},{2,10},{4,12},{6,14},{8,0},{10,2},{12,4},{14,6},{16,24},{18,... | collective-permute-start | bytes 49160 | tf_op jit(solution)/shard_map/ppermute | solution.py:317
  37.6 4.3 %collective-permute-start.12 = (f32[4,8,128]{2,1,0:T(8,128)S(1)}, f32[4,8,128]{2,1,0:T(8,128)S(1)}, u32[]{:S(2)}, u32[]{:S(2)}) collective-permute-start(f32[4,8,128]{2,1,0:T(8,128)S(1)} %shard_map.52.rows_0_), channel_id=1, source_target_pairs={{0,1},{1,0},{2,3},{3,2},{4,5},{5,4},{6,7},{7,6},{8,9},{9,8},{10,11... | collective-permute-start | bytes 49160 | tf_op jit(solution)/shard_map/ppermute | solution.py:320
  38.5 5.1 %collective-permute-start.15 = (f32[4,8,128]{2,1,0:T(8,128)S(1)}, f32[4,8,128]{2,1,0:T(8,128)S(1)}, u32[]{:S(2)}, u32[]{:S(2)}) collective-permute-start(f32[4,8,128]{2,1,0:T(8,128)S(1)} %shard_map.54.cols_0_), channel_id=1, source_target_pairs={{0,16},{2,18},{4,20},{6,22},{8,24},{10,26},{12,28},{14,30},{16,0},... | collective-permute-start | bytes 49160 | tf_op jit(solution)/shard_map/ppermute | solution.py:317
  45.1 3.8 %collective-permute-start.16 = (f32[24,128]{1,0:T(8,128)S(1)}, f32[24,128]{1,0:T(8,128)S(1)}, u32[]{:S(2)}, u32[]{:S(2)}) collective-permute-start(f32[24,128]{1,0:T(8,128)S(1)} %pad_maximum_fusion), channel_id=1, source_target_pairs={{0,4},{2,6},{4,0},{6,2},{8,12},{10,14},{12,8},{14,10},{16,20},{18,... | collective-permute-start | bytes 36872 | tf_op jit(solution)/shard_map/ppermute | solution.py:317
  48.9 3.7 %collective-permute-start.17 = (f32[4,4,128]{2,1,0:T(4,128)S(1)}, f32[4,4,128]{2,1,0:T(4,128)S(1)}, u32[]{:S(2)}, u32[]{:S(2)}) collective-permute-start(f32[4,4,128]{2,1,0:T(4,128)S(1)} %shard_map.57.mine), channel_id=1, source_target_pairs={{0,1},{1,0},{2,3},{3,2},{4,5},{5,4},{6,7},{7,6},{8,9},{9,8},{10,11... | collective-permute-start | bytes 24584 | tf_op jit(solution)/shard_map/ppermute | solution.py:320
where the time goes:
time: 53.4 us; the launch traced here: 53.2 us
  waiting for transfers between devices  22.1 us (41%)
  starting transfers between devices  20.4 us (38%)
  Pallas kernels  6.69 us (13%)
  local copies, waits for them, and re-layouts  3.22 us (6%)
  between operations  0.76 us (1%)
    ppermute x13, waiting for transfers between devices, over_src(): return lax.ppermute(array, 'src', xor_pairs(n_src, mask))  20.3 us
    ppermute x13, starting transfers between devices, over_src(): return lax.ppermute(array, 'src', xor_pairs(n_src, mask))  13.5 us
    pallas_call x10, Pallas kernels, call(): pl.pallas_call(kernel, out_shape=tuple((jax.ShapeDtypeStruct(shape, jnp.f...  6.62 us
    ppermute x2, starting transfers between devices, over_both(): return lax.ppermute(array, ('src', 'tgt'), pairs)  4.55 us
    unnamed x5, local copies, waits for them, and re-layouts  2.6 us
    ppermute x3, starting transfers between devices, over_tgt(): return lax.ppermute(array, 'tgt', xor_pairs(n_tgt, mask))  2.36 us
    ppermute x3, waiting for transfers between devices, over_tgt(): return lax.ppermute(array, 'tgt', xor_pairs(n_tgt, mask))  1.85 us
  transfers between devices with their start and end apart: 18, of which 8 were waited for; matrix products, arithmetic and copies ran while one was open for 1% of the time, Pallas kernels for 8%

commit v1 on v0

--- a/solution.py
+++ b/solution.py
@@ -187,15 +187,16 @@
 
 
 def flipped(ref, k, unit):
-    if unit >= LANES:
-        step = unit // LANES
-        firsts = [line ^ step for line in range(0, ref.shape[1], step)]
-        return jnp.concatenate([ref[k, first : first + step, :] for first in firsts], axis=0)
+    step = unit // LANES
     values = ref[k]
-    if unit:
-        lane = lax.broadcasted_iota(jnp.int32, values.shape, 1)
-        up, down = pltpu.roll(values, LANES - unit, 1), pltpu.roll(values, unit, 1)
-        values = jnp.where((lane & unit) == 0, up, down)
+    if step:
+        lines = [line ^ step for line in range(ref.shape[1])]
+        values = jnp.concatenate([ref[k, line : line + 1, :] for line in lines], axis=0)
+    lane = lax.broadcasted_iota(jnp.int32, values.shape, 1)
+    for bit in bits_below(LANES):
+        if unit & bit:
+            up, down = pltpu.roll(values, LANES - bit, 1), pltpu.roll(values, bit, 1)
+            values = jnp.where((lane & bit) == 0, up, down)
     return values
 
 
@@ -381,13 +382,13 @@
         for bit in bits_below(near):
             row_best = merge_arrays(row_best, over_src(row_best, 2 * bit), bit * rows)
         for bit in bits_below(far)[:-1]:
-            col_best = merge_arrays(col_best, over_src(col_best, 2 * near * bit), 2 * bit * t_rows)
+            col_best = merge_arrays(col_best, over_src(col_best, 2 * near * bit + 1), (2 * bit + 1) * t_rows)
         for bit in bits_below(n_tgt)[:-1]:
             row_best = merge_arrays(row_best, over_tgt(row_best, bit))
         row_pair = [row_best, over_tgt(row_best, n_tgt // 2)]
-        col_pair = [col_best, over_src(col_best, near * far)]
+        col_pair = [col_best, over_src(col_best, near * far + 1)]
         margins, fwd, bwd = call(
-            functools.partial(margin_kernel, far * t_rows),
+            functools.partial(margin_kernel, (far + 1) * t_rows),
             (cosines[0], cosines[1:], cos_late, row_pair, col_pair),
             [(K, src_lines, LANES), (src_lines, LANES), (tgt_lines, LANES)],
             [(block_tgt, LANES), cosines[0].shape], hbm_in=(0,), sems=1,

time: 53.4 us -> 52.5 us (0.983)
  starting transfers between devices: 20.4 us -> 19.8 us
    ppermute x13, starting transfers between devices: 13.5 us -> 12.9 us  [over_src(): return lax.ppermute(array, 'src', xor_pairs(n_src, mask))]
where the time goes in v1:
time: 52.5 us; the launch traced here: 52.3 us
  waiting for transfers between devices  21.8 us (42%)
  starting transfers between devices  19.8 us (38%)
  Pallas kernels  6.71 us (13%)
  local copies, waits for them, and re-layouts  3.22 us (6%)
  between operations  0.76 us (1%)
    ppermute x13, waiting for transfers between devices, over_src(): return lax.ppermute(array, 'src', xor_pairs(n_src, mask))  19.7 us
    ppermute x13, starting transfers between devices, over_src(): return lax.ppermute(array, 'src', xor_pairs(n_src, mask))  12.9 us
    pallas_call x10, Pallas kernels, call(): pl.pallas_call(kernel, out_shape=tuple((jax.ShapeDtypeStruct(shape, jnp.f...  6.64 us
    ppermute x2, starting transfers between devices, over_both(): return lax.ppermute(array, ('src', 'tgt'), pairs)  4.55 us
    unnamed x5, local copies, waits for them, and re-layouts  2.6 us
    ppermute x3, starting transfers between devices, over_tgt(): return lax.ppermute(array, 'tgt', xor_pairs(n_tgt, mask))  2.34 us
    ppermute x3, waiting for transfers between devices, over_tgt(): return lax.ppermute(array, 'tgt', xor_pairs(n_tgt, mask))  2.04 us
  transfers between devices with their start and end apart: 18, of which 8 were waited for; matrix products, arithmetic and copies ran while one was open for 1% of the time, Pallas kernels for 8%

profile of v1, /device:TPU:0, one launch (start us, length us, event | category | flops | bytes accessed | tf_op | source)
XLA Modules:
  0.0 52.3 jit_solution(9738321803315173358)
XLA Ops:
  0.6 3.1 %collective-permute-start = (bf16[512,512]{1,0:T(8,128)(2,1)}, bf16[512,512]{1,0:T(8,128)(2,1)S(1)}, u32[]{:S(2)}, u32[]{:S(2)}) collective-permute-start(bf16[512,512]{1,0:T(8,128)(2,1)} %source.1), channel_id=1, source_target_pairs={{0,1},{1,0},{2,3},{3,2},{4,5},{5,4},{6,7},{7,6},{8,9},{9,8},{10,11... | collective-permute-start | bytes 1572872 | tf_op jit(solution)/shard_map/ppermute | solution.py:325
  3.7 1.5 %collective-permute-start.6 = (bf16[512,512]{1,0:T(8,128)(2,1)}, bf16[512,512]{1,0:T(8,128)(2,1)S(1)}, u32[]{:S(2)}, u32[]{:S(2)}) collective-permute-start(bf16[512,512]{1,0:T(8,128)(2,1)} %source.1), channel_id=1, source_target_pairs={{0,4},{1,5},{2,6},{3,7},{4,0},{5,1},{6,2},{7,3},{8,12},{9,13},{10,... | collective-permute-start | bytes 1572872 | tf_op jit(solution)/shard_map/ppermute | solution.py:325
  5.2 2.6 %collective-permute-start.4 = (bf16[128,1024]{1,0:T(8,128)(2,1)}, bf16[128,1024]{1,0:T(8,128)(2,1)S(1)}, u32[]{:S(2)}, u32[]{:S(2)}) collective-permute-start(bf16[128,1024]{1,0:T(8,128)(2,1)} %target.1), channel_id=1, source_target_pairs={{0,16},{2,18},{4,20},{6,22},{8,24},{10,26},{12,28},{14,30},{16,0},... | collective-permute-start | bytes 786440 | tf_op jit(solution)/shard_map/ppermute | solution.py:318
  7.8 1.6 %collective-permute-start.2 = (bf16[128,1024]{1,0:T(8,128)(2,1)}, bf16[128,1024]{1,0:T(8,128)(2,1)S(1)}, u32[]{:S(2)}, u32[]{:S(2)}) collective-permute-start(bf16[128,1024]{1,0:T(8,128)(2,1)} %target.1), channel_id=1, source_target_pairs={{0,8},{2,10},{4,12},{6,14},{8,0},{10,2},{12,4},{14,6},{16,24},{18,... | collective-permute-start | bytes 786440 | tf_op jit(solution)/shard_map/ppermute | solution.py:318
  9.4 10.1 %collective-permute-done.4.targets_4_ = bf16[128,1024]{1,0:T(8,128)(2,1)S(1)} collective-permute-done((bf16[128,1024]{1,0:T(8,128)(2,1)}, bf16[128,1024]{1,0:T(8,128)(2,1)S(1)}, u32[]{:S(2)}, u32[]{:S(2)}) %collective-permute-start.4) | collective-permute-done | bytes 262176 | tf_op jit(solution)/shard_map/ppermute | solution.py:318
  19.5 0.7 %collective-permute-start.9 = (bf16[128,1024]{1,0:T(8,128)(2,1)S(1)}, bf16[128,1024]{1,0:T(8,128)(2,1)S(1)}, u32[]{:S(2)}, u32[]{:S(2)}) collective-permute-start(bf16[128,1024]{1,0:T(8,128)(2,1)S(1)} %collective-permute-done.4.targets_4_), channel_id=1, source_target_pairs={{0,8},{2,10},{4,12},{6,14},{8,0},{10,2},{12,4},{14,6},{16,24},{18,... | collective-permute-start | bytes 786440 | tf_op jit(solution)/shard_map/ppermute | solution.py:318
  20.2 0.5 collective-permute-start.3
  20.7 0.6 %collective-permute-start.7 = (bf16[256,512]{1,0:T(8,128)(2,1)S(1)}, bf16[256,512]{1,0:T(8,128)(2,1)S(1)}, u32[]{:S(2)}, u32[]{:S(2)}) collective-permute-start(bf16[256,512]{1,0:T(8,128)(2,1)S(1)} %slice.28), channel_id=1, source_target_pairs={{0,4},{2,6},{4,0},{6,2},{8,12},{10,14},{12,8},{14,10},{16,20},{18,... | collective-permute-start | bytes 786440 | tf_op jit(solution)/shard_map/ppermute | solution.py:318
  21.4 0.6 %collective-permute-start.8 = (bf16[256,512]{1,0:T(8,128)(2,1)S(1)}, bf16[256,512]{1,0:T(8,128)(2,1)S(1)}, u32[]{:S(2)}, u32[]{:S(2)}) collective-permute-start(bf16[256,512]{1,0:T(8,128)(2,1)S(1)} %slice.29), channel_id=1, source_target_pairs={{0,1},{1,0},{2,3},{3,2},{4,5},{5,4},{6,7},{7,6},{8,9},{9,8},{10,11... | collective-permute-start | bytes 786440 | tf_op jit(solution)/shard_map/ppermute | solution.py:321
  21.9 4.7 %collective-permute-done.9.targets_0_ = bf16[128,1024]{1,0:T(8,128)(2,1)S(1)} collective-permute-done((bf16[128,1024]{1,0:T(8,128)(2,1)S(1)}, bf16[128,1024]{1,0:T(8,128)(2,1)S(1)}, u32[]{:S(2)}, u32[]{:S(2)}) %collective-permute-start.9) | collective-permute-done | bytes 262176 | tf_op jit(solution)/shard_map/ppermute | solution.py:318
  26.7 1.0 %copy-done = bf16[512,512]{1,0:T(8,128)(2,1)S(1)} copy-done((bf16[512,512]{1,0:T(8,128)(2,1)S(1)}, bf16[512,512]{1,0:T(8,128)(2,1)}, u32[]{:S(2)}) %copy-start) | copy-done | bytes 524312
  27.7 0.9 %copy-done.1 = bf16[128,1024]{1,0:T(8,128)(2,1)S(1)} copy-done((bf16[128,1024]{1,0:T(8,128)(2,1)S(1)}, bf16[128,1024]{1,0:T(8,128)(2,1)}, u32[]{:S(2)}) %copy-start.1) | copy-done | bytes 262168
  28.8 1.8 %shard_map.49 = (f32[768,512]{1,0:T(8,128)S(1)}, f32[8,512]{1,0:T(8,128)S(1)}, f32[768,128]{1,0:T(8,128)S(1)}, f32[4,8,512]{2,1,0:T(8,128)S(1)}, f32[4,8,768]{2,1,0:T(8,128)S(1)}) custom-call(bf16[512,512]{1,0:T(8,128)(2,1)S(1)} %get-tuple-element.20.piece_0__0_.pieces_0__0__0_, bf16[512,512]{1,0:T(8,128)(2,1)S(1)} %collective-permute-done.piece_1__0_.pieces_0__1__0_, ...), custom_call_target="tpu_custom_call" | custom-call | flops 805306368 | tf_op jit(solution)/shard_map/pallas_call | solution.py:267
  30.5 1.6 %shard_map.50 = (f32[768,512]{1,0:T(8,128)S(1)}, f32[8,512]{1,0:T(8,128)S(1)}, f32[4,8,512]{2,1,0:T(8,128)S(1)}, f32[4,8,768]{2,1,0:T(8,128)S(1)}) custom-call(bf16[512,512]{1,0:T(8,128)(2,1)S(1)} %collective-permute-done.6.piece_0__0_.pieces_1__0__0_, bf16[256,512]{1,0:T(8,128)(2,1)S(1)} %collective-permute-done.7.piece_1__0_.pieces_1__1__0_, ...), custom_call_target="tpu_custom_call" | custom-call | flops 805306368 | tf_op jit(solution)/shard_map/pallas_call | solution.py:267
  32.2 1.1 %shard_map.51 = (f32[256,1024]{1,0:T(8,128)S(1)}, f32[4,8,128]{2,1,0:T(8,128)S(1)}, f32[4,8,128]{2,1,0:T(8,128)S(1)}) custom-call(bf16[512,512]{1,0:T(8,128)(2,1)S(1)} %get-tuple-element.20.piece_0__0_.pieces_0__0__0_, bf16[512,512]{1,0:T(8,128)(2,1)S(1)} %collective-permute-done.piece_1__0_.pieces_0__1__0_, ...), custom_call_target="tpu_custom_call" | custom-call | flops 536870912 | tf_op jit(solution)/shard_map/pallas_call | solution.py:267
  33.3 0.6 %collective-permute-start.13 = (f32[4,8,128]{2,1,0:T(8,128)S(1)}, f32[4,8,128]{2,1,0:T(8,128)S(1)}, u32[]{:S(2)}, u32[]{:S(2)}) collective-permute-start(f32[4,8,128]{2,1,0:T(8,128)S(1)} %get-tuple-element.33.mine), channel_id=1, source_target_pairs={{0,2},{2,0},{4,6},{6,4},{8,10},{10,8},{12,14},{14,12},{16,18},{18,... | collective-permute-start | bytes 49160 | tf_op jit(solution)/shard_map/ppermute | solution.py:318
  33.9 0.5 %collective-permute-start.11 = (f32[4,8,128]{2,1,0:T(8,128)S(1)}, f32[4,8,128]{2,1,0:T(8,128)S(1)}, u32[]{:S(2)}, u32[]{:S(2)}) collective-permute-start(f32[4,8,128]{2,1,0:T(8,128)S(1)} %get-tuple-element.32.mine), channel_id=1, source_target_pairs={{0,4},{2,6},{4,0},{6,2},{8,12},{10,14},{12,8},{14,10},{16,20},{18,... | collective-permute-start | bytes 49160 | tf_op jit(solution)/shard_map/ppermute | solution.py:318
  34.4 0.3 collective-permute-done.13.arrived
  34.7 1.8 %collective-permute-start.14 = (f32[4,8,128]{2,1,0:T(8,128)S(1)}, f32[4,8,128]{2,1,0:T(8,128)S(1)}, u32[]{:S(2)}, u32[]{:S(2)}) collective-permute-start(f32[4,8,128]{2,1,0:T(8,128)S(1)} %shard_map.53.mine), channel_id=1, source_target_pairs={{0,10},{2,8},{4,14},{6,12},{8,2},{10,0},{12,6},{14,4},{16,26},{18,... | collective-permute-start | bytes 49160 | tf_op jit(solution)/shard_map/ppermute | solution.py:318
  36.5 1.1 %collective-permute-done.11.arrived = f32[4,8,128]{2,1,0:T(8,128)S(1)} collective-permute-done((f32[4,8,128]{2,1,0:T(8,128)S(1)}, f32[4,8,128]{2,1,0:T(8,128)S(1)}, u32[]{:S(2)}, u32[]{:S(2)}) %collective-permute-start.11) | collective-permute-done | bytes 16416 | tf_op jit(solution)/shard_map/ppermute | solution.py:318
  37.6 0.6 %collective-permute-start.12 = (f32[4,8,128]{2,1,0:T(8,128)S(1)}, f32[4,8,128]{2,1,0:T(8,128)S(1)}, u32[]{:S(2)}, u32[]{:S(2)}) collective-permute-start(f32[4,8,128]{2,1,0:T(8,128)S(1)} %shard_map.52.rows_0_), channel_id=1, source_target_pairs={{0,1},{1,0},{2,3},{3,2},{4,5},{5,4},{6,7},{7,6},{8,9},{9,8},{10,11... | collective-permute-start | bytes 49160 | tf_op jit(solution)/shard_map/ppermute | solution.py:321
  38.2 3.1 %collective-permute-start.15 = (f32[4,8,128]{2,1,0:T(8,128)S(1)}, f32[4,8,128]{2,1,0:T(8,128)S(1)}, u32[]{:S(2)}, u32[]{:S(2)}) collective-permute-start(f32[4,8,128]{2,1,0:T(8,128)S(1)} %shard_map.54.cols_0_), channel_id=1, source_target_pairs={{0,18},{2,16},{4,22},{6,20},{8,26},{10,24},{12,30},{14,28},{16,2},... | collective-permute-start | bytes 49160 | tf_op jit(solution)/shard_map/ppermute | solution.py:318
  41.3 0.2 collective-permute-done.12.rows_1_
  41.4 1.3 %collective-permute-done.15.cols_1_ = f32[4,8,128]{2,1,0:T(8,128)S(1)} collective-permute-done((f32[4,8,128]{2,1,0:T(8,128)S(1)}, f32[4,8,128]{2,1,0:T(8,128)S(1)}, u32[]{:S(2)}, u32[]{:S(2)}) %collective-permute-start.15) | collective-permute-done | bytes 16416 | tf_op jit(solution)/shard_map/ppermute | solution.py:318
  42.7 1.5 %shard_map.55 = (f32[4,8,128]{2,1,0:T(8,128)S(1)}, f32[8,128]{1,0:T(8,128)S(1)}, f32[8,128]{1,0:T(8,128)S(1)}) custom-call(f32[768,512]{1,0:T(8,128)S(1)} %get-tuple-element.22.first, f32[768,512]{1,0:T(8,128)S(1)} %get-tuple-element.25.early_0_, f32[256,1024]{1,0:T(8,128)S(1)} %get-tuple-element.31.late, f32[4,8,128]{2,1,0:T(8,128)S(1)} %shard_map.52.rows_0_, ...), custom_call_target="tpu_custom_call" | custom-call | tf_op jit(solution)/shard_map/pallas_call | solution.py:267
  44.2 1.0 %collective-permute-start.16 = (f32[24,128]{1,0:T(8,128)S(1)}, f32[24,128]{1,0:T(8,128)S(1)}, u32[]{:S(2)}, u32[]{:S(2)}) collective-permute-start(f32[24,128]{1,0:T(8,128)S(1)} %pad_maximum_fusion), channel_id=1, source_target_pairs={{0,4},{2,6},{4,0},{6,2},{8,12},{10,14},{12,8},{14,10},{16,20},{18,... | collective-permute-start | bytes 36872 | tf_op jit(solution)/shard_map/ppermute | solution.py:318
  45.2 0.6 %slice_bitcast_fusion.2 = f32[512]{0:T(512)} fusion(f32[8,128]{1,0:T(8,128)S(1)} %get-tuple-element.34), kind=kLoop, calls=%fused_computation.5 | loop fusion | bytes 4096 | tf_op jit(solution)/shard_map/reshape | solution.py:422
  45.8 2.2 %collective-permute-done.16 = f32[24,128]{1,0:T(8,128)S(1)} collective-permute-done((f32[24,128]{1,0:T(8,128)S(1)}, f32[24,128]{1,0:T(8,128)S(1)}, u32[]{:S(2)}, u32[]{:S(2)}) %collective-permute-start.16) | collective-permute-done | bytes 12320 | tf_op jit(solution)/shard_map/ppermute | solution.py:318
  48.0 1.2 %collective-permute-start.17 = (f32[4,4,128]{2,1,0:T(4,128)S(1)}, f32[4,4,128]{2,1,0:T(4,128)S(1)}, u32[]{:S(2)}, u32[]{:S(2)}) collective-permute-start(f32[4,4,128]{2,1,0:T(4,128)S(1)} %shard_map.57.mine), channel_id=1, source_target_pairs={{0,1},{1,0},{2,3},{3,2},{4,5},{5,4},{6,7},{7,6},{8,9},{9,8},{10,11... | collective-permute-start | bytes 24584 | tf_op jit(solution)/shard_map/ppermute | solution.py:321
  49.2 0.6 %shard_map.56 = f32[16,128]{1,0:T(8,128)} custom-call(f32[16,128]{1,0:T(8,128)S(1)} %maximum_bitcast_fusion.known), custom_call_target="tpu_custom_call" | custom-call | tf_op jit(solution)/shard_map/pallas_call | solution.py:267
  49.8 1.9 %collective-permute-done.17.arrived = f32[4,4,128]{2,1,0:T(4,128)S(1)} collective-permute-done((f32[4,4,128]{2,1,0:T(4,128)S(1)}, f32[4,4,128]{2,1,0:T(4,128)S(1)}, u32[]{:S(2)}, u32[]{:S(2)}) %collective-permute-start.17) | collective-permute-done | bytes 8224 | tf_op jit(solution)/shard_map/ppermute | solution.py:321
  51.7 0.6 %copy.9 = f32[1,4,4,128]{3,1,2,0:T(4,128)} copy(f32[1,4,4,128]{3,2,1,0:T(4,128)S(1)} %bitcast.20) | data formatting | bytes 16384
  (28 shorter events, 0.2 us)
Async XLA Ops:
  0.6 19.6 %collective-permute-start = (bf16[512,512]{1,0:T(8,128)(2,1)}, bf16[512,512]{1,0:T(8,128)(2,1)S(1)}, u32[]{:S(2)}, u32[]{:S(2)}) collective-permute-start(bf16[512,512]{1,0:T(8,128)(2,1)} %source.1), channel_id=1, source_target_pairs={{0,1},{1,0},{2,3},{3,2},{4,5},{5,4},{6,7},{7,6},{8,9},{9,8},{10,11... | collective-permute-start | bytes 1572872 | tf_op jit(solution)/shard_map/ppermute | solution.py:325
  3.7 17.0 %collective-permute-start.6 = (bf16[512,512]{1,0:T(8,128)(2,1)}, bf16[512,512]{1,0:T(8,128)(2,1)S(1)}, u32[]{:S(2)}, u32[]{:S(2)}) collective-permute-start(bf16[512,512]{1,0:T(8,128)(2,1)} %source.1), channel_id=1, source_target_pairs={{0,4},{1,5},{2,6},{3,7},{4,0},{5,1},{6,2},{7,3},{8,12},{9,13},{10,... | collective-permute-start | bytes 1572872 | tf_op jit(solution)/shard_map/ppermute | solution.py:325
  5.2 14.3 %collective-permute-start.4 = (bf16[128,1024]{1,0:T(8,128)(2,1)}, bf16[128,1024]{1,0:T(8,128)(2,1)S(1)}, u32[]{:S(2)}, u32[]{:S(2)}) collective-permute-start(bf16[128,1024]{1,0:T(8,128)(2,1)} %target.1), channel_id=1, source_target_pairs={{0,16},{2,18},{4,20},{6,22},{8,24},{10,26},{12,28},{14,30},{16,0},... | collective-permute-start | bytes 786440 | tf_op jit(solution)/shard_map/ppermute | solution.py:318
  7.8 12.4 %collective-permute-start.2 = (bf16[128,1024]{1,0:T(8,128)(2,1)}, bf16[128,1024]{1,0:T(8,128)(2,1)S(1)}, u32[]{:S(2)}, u32[]{:S(2)}) collective-permute-start(bf16[128,1024]{1,0:T(8,128)(2,1)} %target.1), channel_id=1, source_target_pairs={{0,8},{2,10},{4,12},{6,14},{8,0},{10,2},{12,4},{14,6},{16,24},{18,... | collective-permute-start | bytes 786440 | tf_op jit(solution)/shard_map/ppermute | solution.py:318
  9.3 12.0 %collective-permute-start.1 = (bf16[128,1024]{1,0:T(8,128)(2,1)}, bf16[128,1024]{1,0:T(8,128)(2,1)S(1)}, u32[]{:S(2)}, u32[]{:S(2)}) collective-permute-start(bf16[128,1024]{1,0:T(8,128)(2,1)} %target.1), channel_id=1, source_target_pairs={{0,2},{2,0},{4,6},{6,4},{8,10},{10,8},{12,14},{14,12},{16,18},{18,... | collective-permute-start | bytes 786440 | tf_op jit(solution)/shard_map/ppermute | solution.py:318
  19.5 7.2 %collective-permute-start.9 = (bf16[128,1024]{1,0:T(8,128)(2,1)S(1)}, bf16[128,1024]{1,0:T(8,128)(2,1)S(1)}, u32[]{:S(2)}, u32[]{:S(2)}) collective-permute-start(bf16[128,1024]{1,0:T(8,128)(2,1)S(1)} %collective-permute-done.4.targets_4_), channel_id=1, source_target_pairs={{0,8},{2,10},{4,12},{6,14},{8,0},{10,2},{12,4},{14,6},{16,24},{18,... | collective-permute-start | bytes 786440 | tf_op jit(solution)/shard_map/ppermute | solution.py:318
  20.2 8.6 %collective-permute-start.5 = (bf16[128,1024]{1,0:T(8,128)(2,1)S(1)}, bf16[128,1024]{1,0:T(8,128)(2,1)S(1)}, u32[]{:S(2)}, u32[]{:S(2)}) collective-permute-start(bf16[128,1024]{1,0:T(8,128)(2,1)S(1)} %collective-permute-done.4.targets_4_), channel_id=1, source_target_pairs={{0,2},{2,0},{4,6},{6,4},{8,10},{10,8},{12,14},{14,12},{16,18},{18,... | collective-permute-start | bytes 786440 | tf_op jit(solution)/shard_map/ppermute | solution.py:318
  20.2 8.6 %collective-permute-start.3 = (bf16[128,1024]{1,0:T(8,128)(2,1)S(1)}, bf16[128,1024]{1,0:T(8,128)(2,1)S(1)}, u32[]{:S(2)}, u32[]{:S(2)}) collective-permute-start(bf16[128,1024]{1,0:T(8,128)(2,1)S(1)} %collective-permute-done.2.targets_2_), channel_id=1, source_target_pairs={{0,2},{2,0},{4,6},{6,4},{8,10},{10,8},{12,14},{14,12},{16,18},{18,... | collective-permute-start | bytes 786440 | tf_op jit(solution)/shard_map/ppermute | solution.py:318
  20.7 9.8 %collective-permute-start.7 = (bf16[256,512]{1,0:T(8,128)(2,1)S(1)}, bf16[256,512]{1,0:T(8,128)(2,1)S(1)}, u32[]{:S(2)}, u32[]{:S(2)}) collective-permute-start(bf16[256,512]{1,0:T(8,128)(2,1)S(1)} %slice.28), channel_id=1, source_target_pairs={{0,4},{2,6},{4,0},{6,2},{8,12},{10,14},{12,8},{14,10},{16,20},{18,... | collective-permute-start | bytes 786440 | tf_op jit(solution)/shard_map/ppermute | solution.py:318
  21.4 9.2 %collective-permute-start.8 = (bf16[256,512]{1,0:T(8,128)(2,1)S(1)}, bf16[256,512]{1,0:T(8,128)(2,1)S(1)}, u32[]{:S(2)}, u32[]{:S(2)}) collective-permute-start(bf16[256,512]{1,0:T(8,128)(2,1)S(1)} %slice.29), channel_id=1, source_target_pairs={{0,1},{1,0},{2,3},{3,2},{4,5},{5,4},{6,7},{7,6},{8,9},{9,8},{10,11... | collective-permute-start | bytes 786440 | tf_op jit(solution)/shard_map/ppermute | solution.py:321
  26.7 5.5 %collective-permute-start.10 = (bf16[128,1024]{1,0:T(8,128)(2,1)S(1)}, bf16[128,1024]{1,0:T(8,128)(2,1)S(1)}, u32[]{:S(2)}, u32[]{:S(2)}) collective-permute-start(bf16[128,1024]{1,0:T(8,128)(2,1)S(1)} %collective-permute-done.9.targets_0_), channel_id=1, source_target_pairs={{0,2},{2,0},{4,6},{6,4},{8,10},{10,8},{12,14},{14,12},{16,18},{18,... | collective-permute-start | bytes 786440 | tf_op jit(solution)/shard_map/ppermute | solution.py:318
  26.7 1.0 %copy-start = (bf16[512,512]{1,0:T(8,128)(2,1)S(1)}, bf16[512,512]{1,0:T(8,128)(2,1)}, u32[]{:S(2)}) copy-start(bf16[512,512]{1,0:T(8,128)(2,1)} %source.1) | copy-start | bytes 1572868
  27.7 0.9 %copy-start.1 = (bf16[128,1024]{1,0:T(8,128)(2,1)S(1)}, bf16[128,1024]{1,0:T(8,128)(2,1)}, u32[]{:S(2)}) copy-start(bf16[128,1024]{1,0:T(8,128)(2,1)} %target.1) | copy-start | bytes 786436
  33.3 1.4 %collective-permute-start.13 = (f32[4,8,128]{2,1,0:T(8,128)S(1)}, f32[4,8,128]{2,1,0:T(8,128)S(1)}, u32[]{:S(2)}, u32[]{:S(2)}) collective-permute-start(f32[4,8,128]{2,1,0:T(8,128)S(1)} %get-tuple-element.33.mine), channel_id=1, source_target_pairs={{0,2},{2,0},{4,6},{6,4},{8,10},{10,8},{12,14},{14,12},{16,18},{18,... | collective-permute-start | bytes 49160 | tf_op jit(solution)/shard_map/ppermute | solution.py:318
  33.9 3.7 %collective-permute-start.11 = (f32[4,8,128]{2,1,0:T(8,128)S(1)}, f32[4,8,128]{2,1,0:T(8,128)S(1)}, u32[]{:S(2)}, u32[]{:S(2)}) collective-permute-start(f32[4,8,128]{2,1,0:T(8,128)S(1)} %get-tuple-element.32.mine), channel_id=1, source_target_pairs={{0,4},{2,6},{4,0},{6,2},{8,12},{10,14},{12,8},{14,10},{16,20},{18,... | collective-permute-start | bytes 49160 | tf_op jit(solution)/shard_map/ppermute | solution.py:318
  34.7 3.5 %collective-permute-start.14 = (f32[4,8,128]{2,1,0:T(8,128)S(1)}, f32[4,8,128]{2,1,0:T(8,128)S(1)}, u32[]{:S(2)}, u32[]{:S(2)}) collective-permute-start(f32[4,8,128]{2,1,0:T(8,128)S(1)} %shard_map.53.mine), channel_id=1, source_target_pairs={{0,10},{2,8},{4,14},{6,12},{8,2},{10,0},{12,6},{14,4},{16,26},{18,... | collective-permute-start | bytes 49160 | tf_op jit(solution)/shard_map/ppermute | solution.py:318
  37.6 3.8 %collective-permute-start.12 = (f32[4,8,128]{2,1,0:T(8,128)S(1)}, f32[4,8,128]{2,1,0:T(8,128)S(1)}, u32[]{:S(2)}, u32[]{:S(2)}) collective-permute-start(f32[4,8,128]{2,1,0:T(8,128)S(1)} %shard_map.52.rows_0_), channel_id=1, source_target_pairs={{0,1},{1,0},{2,3},{3,2},{4,5},{5,4},{6,7},{7,6},{8,9},{9,8},{10,11... | collective-permute-start | bytes 49160 | tf_op jit(solution)/shard_map/ppermute | solution.py:321
  38.2 4.5 %collective-permute-start.15 = (f32[4,8,128]{2,1,0:T(8,128)S(1)}, f32[4,8,128]{2,1,0:T(8,128)S(1)}, u32[]{:S(2)}, u32[]{:S(2)}) collective-permute-start(f32[4,8,128]{2,1,0:T(8,128)S(1)} %shard_map.54.cols_0_), channel_id=1, source_target_pairs={{0,18},{2,16},{4,22},{6,20},{8,26},{10,24},{12,30},{14,28},{16,2},... | collective-permute-start | bytes 49160 | tf_op jit(solution)/shard_map/ppermute | solution.py:318
  44.2 3.8 %collective-permute-start.16 = (f32[24,128]{1,0:T(8,128)S(1)}, f32[24,128]{1,0:T(8,128)S(1)}, u32[]{:S(2)}, u32[]{:S(2)}) collective-permute-start(f32[24,128]{1,0:T(8,128)S(1)} %pad_maximum_fusion), channel_id=1, source_target_pairs={{0,4},{2,6},{4,0},{6,2},{8,12},{10,14},{12,8},{14,10},{16,20},{18,... | collective-permute-start | bytes 36872 | tf_op jit(solution)/shard_map/ppermute | solution.py:318
  48.0 3.7 %collective-permute-start.17 = (f32[4,4,128]{2,1,0:T(4,128)S(1)}, f32[4,4,128]{2,1,0:T(4,128)S(1)}, u32[]{:S(2)}, u32[]{:S(2)}) collective-permute-start(f32[4,4,128]{2,1,0:T(4,128)S(1)} %shard_map.57.mine), channel_id=1, source_target_pairs={{0,1},{1,0},{2,3},{3,2},{4,5},{5,4},{6,7},{7,6},{8,9},{9,8},{10,11... | collective-permute-start | bytes 24584 | tf_op jit(solution)/shard_map/ppermute | solution.py:321

commit v2 on v1

--- a/solution.py
+++ b/solution.py
@@ -378,15 +378,21 @@
             [(l_rows, block_src), (l_rows, LANES)], 2 * l_rows * block_src * width,
         )
 
-        col_best = merge_arrays(col_best, over_src(col_best, 1), t_rows)
+        arrived = over_src(col_best, 1)
+        col_best = merge_arrays(col_best, arrived, t_rows)
         for bit in bits_below(near):
-            row_best = merge_arrays(row_best, over_src(row_best, 2 * bit), bit * rows)
-        for bit in bits_below(far)[:-1]:
-            col_best = merge_arrays(col_best, over_src(col_best, 2 * near * bit + 1), (2 * bit + 1) * t_rows)
-        for bit in bits_below(n_tgt)[:-1]:
-            row_best = merge_arrays(row_best, over_tgt(row_best, bit))
-        row_pair = [row_best, over_tgt(row_best, n_tgt // 2)]
-        col_pair = [col_best, over_src(col_best, near * far + 1)]
+            arrived = over_src(row_best, 2 * bit)
+            row_best = merge_arrays(row_best, arrived, bit * rows)
+        for bit in bits_below(n_tgt):
+            arrived = over_tgt(row_best, bit)
+            if 2 * bit < n_tgt:
+                row_best = merge_arrays(row_best, arrived)
+        row_pair = [row_best, arrived]
+        for bit in bits_below(far):
+            arrived = over_src(col_best, 2 * near * bit + 1)
+            if 2 * bit < far:
+                col_best = merge_arrays(col_best, arrived, (2 * bit + 1) * t_rows)
+        col_pair = [col_best, arrived]
         margins, fwd, bwd = call(
             functools.partial(margin_kernel, (far + 1) * t_rows),
             (cosines[0], cosines[1:], cos_late, row_pair, col_pair),

time: 52.5 us -> 52.5 us (level)
  no operation moved by 1% of the time
where the time goes in v2:
time: 52.5 us; the launch traced here: 52.3 us
  waiting for transfers between devices  21.8 us (42%)
  starting transfers between devices  19.8 us (38%)
  Pallas kernels  6.71 us (13%)
  local copies, waits for them, and re-layouts  3.22 us (6%)
  between operations  0.76 us (1%)
    ppermute x13, waiting for transfers between devices, over_src(): return lax.ppermute(array, 'src', xor_pairs(n_src, mask))  19.7 us
    ppermute x13, starting transfers between devices, over_src(): return lax.ppermute(array, 'src', xor_pairs(n_src, mask))  12.9 us
    pallas_call x10, Pallas kernels, call(): pl.pallas_call(kernel, out_shape=tuple((jax.ShapeDtypeStruct(shape, jnp.f...  6.64 us
    ppermute x2, starting transfers between devices, over_both(): return lax.ppermute(array, ('src', 'tgt'), pairs)  4.55 us
    unnamed x5, local copies, waits for them, and re-layouts  2.6 us
    ppermute x3, starting transfers between devices, over_tgt(): return lax.ppermute(array, 'tgt', xor_pairs(n_tgt, mask))  2.34 us
    ppermute x3, waiting for transfers between devices, over_tgt(): return lax.ppermute(array, 'tgt', xor_pairs(n_tgt, mask))  2.04 us
  transfers between devices with their start and end apart: 18, of which 8 were waited for; matrix products, arithmetic and copies ran while one was open for 1% of the time, Pallas kernels for 8%

profile of v2, /device:TPU:0, one launch (start us, length us, event | category | flops | bytes accessed | tf_op | source)
XLA Modules:
  0.0 52.3 jit_solution(9738321803315173358)
XLA Ops:
  0.6 3.1 %collective-permute-start = (bf16[512,512]{1,0:T(8,128)(2,1)}, bf16[512,512]{1,0:T(8,128)(2,1)S(1)}, u32[]{:S(2)}, u32[]{:S(2)}) collective-permute-start(bf16[512,512]{1,0:T(8,128)(2,1)} %source.1), channel_id=1, source_target_pairs={{0,1},{1,0},{2,3},{3,2},{4,5},{5,4},{6,7},{7,6},{8,9},{9,8},{10,11... | collective-permute-start | bytes 1572872 | tf_op jit(solution)/shard_map/ppermute | solution.py:325
  3.7 1.5 %collective-permute-start.6 = (bf16[512,512]{1,0:T(8,128)(2,1)}, bf16[512,512]{1,0:T(8,128)(2,1)S(1)}, u32[]{:S(2)}, u32[]{:S(2)}) collective-permute-start(bf16[512,512]{1,0:T(8,128)(2,1)} %source.1), channel_id=1, source_target_pairs={{0,4},{1,5},{2,6},{3,7},{4,0},{5,1},{6,2},{7,3},{8,12},{9,13},{10,... | collective-permute-start | bytes 1572872 | tf_op jit(solution)/shard_map/ppermute | solution.py:325
  5.2 2.6 %collective-permute-start.4 = (bf16[128,1024]{1,0:T(8,128)(2,1)}, bf16[128,1024]{1,0:T(8,128)(2,1)S(1)}, u32[]{:S(2)}, u32[]{:S(2)}) collective-permute-start(bf16[128,1024]{1,0:T(8,128)(2,1)} %target.1), channel_id=1, source_target_pairs={{0,16},{2,18},{4,20},{6,22},{8,24},{10,26},{12,28},{14,30},{16,0},... | collective-permute-start | bytes 786440 | tf_op jit(solution)/shard_map/ppermute | solution.py:318
  7.8 1.6 %collective-permute-start.2 = (bf16[128,1024]{1,0:T(8,128)(2,1)}, bf16[128,1024]{1,0:T(8,128)(2,1)S(1)}, u32[]{:S(2)}, u32[]{:S(2)}) collective-permute-start(bf16[128,1024]{1,0:T(8,128)(2,1)} %target.1), channel_id=1, source_target_pairs={{0,8},{2,10},{4,12},{6,14},{8,0},{10,2},{12,4},{14,6},{16,24},{18,... | collective-permute-start | bytes 786440 | tf_op jit(solution)/shard_map/ppermute | solution.py:318
  9.4 10.1 %collective-permute-done.4.targets_4_ = bf16[128,1024]{1,0:T(8,128)(2,1)S(1)} collective-permute-done((bf16[128,1024]{1,0:T(8,128)(2,1)}, bf16[128,1024]{1,0:T(8,128)(2,1)S(1)}, u32[]{:S(2)}, u32[]{:S(2)}) %collective-permute-start.4) | collective-permute-done | bytes 262176 | tf_op jit(solution)/shard_map/ppermute | solution.py:318
  19.5 0.7 %collective-permute-start.9 = (bf16[128,1024]{1,0:T(8,128)(2,1)S(1)}, bf16[128,1024]{1,0:T(8,128)(2,1)S(1)}, u32[]{:S(2)}, u32[]{:S(2)}) collective-permute-start(bf16[128,1024]{1,0:T(8,128)(2,1)S(1)} %collective-permute-done.4.targets_4_), channel_id=1, source_target_pairs={{0,8},{2,10},{4,12},{6,14},{8,0},{10,2},{12,4},{14,6},{16,24},{18,... | collective-permute-start | bytes 786440 | tf_op jit(solution)/shard_map/ppermute | solution.py:318
  20.2 0.5 collective-permute-start.3
  20.7 0.6 %collective-permute-start.7 = (bf16[256,512]{1,0:T(8,128)(2,1)S(1)}, bf16[256,512]{1,0:T(8,128)(2,1)S(1)}, u32[]{:S(2)}, u32[]{:S(2)}) collective-permute-start(bf16[256,512]{1,0:T(8,128)(2,1)S(1)} %slice.28), channel_id=1, source_target_pairs={{0,4},{2,6},{4,0},{6,2},{8,12},{10,14},{12,8},{14,10},{16,20},{18,... | collective-permute-start | bytes 786440 | tf_op jit(solution)/shard_map/ppermute | solution.py:318
  21.4 0.6 %collective-permute-start.8 = (bf16[256,512]{1,0:T(8,128)(2,1)S(1)}, bf16[256,512]{1,0:T(8,128)(2,1)S(1)}, u32[]{:S(2)}, u32[]{:S(2)}) collective-permute-start(bf16[256,512]{1,0:T(8,128)(2,1)S(1)} %slice.29), channel_id=1, source_target_pairs={{0,1},{1,0},{2,3},{3,2},{4,5},{5,4},{6,7},{7,6},{8,9},{9,8},{10,11... | collective-permute-start | bytes 786440 | tf_op jit(solution)/shard_map/ppermute | solution.py:321
  21.9 4.7 %collective-permute-done.9.targets_0_ = bf16[128,1024]{1,0:T(8,128)(2,1)S(1)} collective-permute-done((bf16[128,1024]{1,0:T(8,128)(2,1)S(1)}, bf16[128,1024]{1,0:T(8,128)(2,1)S(1)}, u32[]{:S(2)}, u32[]{:S(2)}) %collective-permute-start.9) | collective-permute-done | bytes 262176 | tf_op jit(solution)/shard_map/ppermute | solution.py:318
  26.7 1.0 %copy-done = bf16[512,512]{1,0:T(8,128)(2,1)S(1)} copy-done((bf16[512,512]{1,0:T(8,128)(2,1)S(1)}, bf16[512,512]{1,0:T(8,128)(2,1)}, u32[]{:S(2)}) %copy-start) | copy-done | bytes 524312
  27.7 0.9 %copy-done.1 = bf16[128,1024]{1,0:T(8,128)(2,1)S(1)} copy-done((bf16[128,1024]{1,0:T(8,128)(2,1)S(1)}, bf16[128,1024]{1,0:T(8,128)(2,1)}, u32[]{:S(2)}) %copy-start.1) | copy-done | bytes 262168
  28.8 1.8 %shard_map.49 = (f32[768,512]{1,0:T(8,128)S(1)}, f32[8,512]{1,0:T(8,128)S(1)}, f32[768,128]{1,0:T(8,128)S(1)}, f32[4,8,512]{2,1,0:T(8,128)S(1)}, f32[4,8,768]{2,1,0:T(8,128)S(1)}) custom-call(bf16[512,512]{1,0:T(8,128)(2,1)S(1)} %get-tuple-element.20.piece_0__0_.pieces_0__0__0_, bf16[512,512]{1,0:T(8,128)(2,1)S(1)} %collective-permute-done.piece_1__0_.pieces_0__1__0_, ...), custom_call_target="tpu_custom_call" | custom-call | flops 805306368 | tf_op jit(solution)/shard_map/pallas_call | solution.py:267
  30.5 1.6 %shard_map.50 = (f32[768,512]{1,0:T(8,128)S(1)}, f32[8,512]{1,0:T(8,128)S(1)}, f32[4,8,512]{2,1,0:T(8,128)S(1)}, f32[4,8,768]{2,1,0:T(8,128)S(1)}) custom-call(bf16[512,512]{1,0:T(8,128)(2,1)S(1)} %collective-permute-done.6.piece_0__0_.pieces_1__0__0_, bf16[256,512]{1,0:T(8,128)(2,1)S(1)} %collective-permute-done.7.piece_1__0_.pieces_1__1__0_, ...), custom_call_target="tpu_custom_call" | custom-call | flops 805306368 | tf_op jit(solution)/shard_map/pallas_call | solution.py:267
  32.2 1.1 %shard_map.51 = (f32[256,1024]{1,0:T(8,128)S(1)}, f32[4,8,128]{2,1,0:T(8,128)S(1)}, f32[4,8,128]{2,1,0:T(8,128)S(1)}) custom-call(bf16[512,512]{1,0:T(8,128)(2,1)S(1)} %get-tuple-element.20.piece_0__0_.pieces_0__0__0_, bf16[512,512]{1,0:T(8,128)(2,1)S(1)} %collective-permute-done.piece_1__0_.pieces_0__1__0_, ...), custom_call_target="tpu_custom_call" | custom-call | flops 536870912 | tf_op jit(solution)/shard_map/pallas_call | solution.py:267
  33.3 0.6 %collective-permute-start.13 = (f32[4,8,128]{2,1,0:T(8,128)S(1)}, f32[4,8,128]{2,1,0:T(8,128)S(1)}, u32[]{:S(2)}, u32[]{:S(2)}) collective-permute-start(f32[4,8,128]{2,1,0:T(8,128)S(1)} %get-tuple-element.33.mine), channel_id=1, source_target_pairs={{0,2},{2,0},{4,6},{6,4},{8,10},{10,8},{12,14},{14,12},{16,18},{18,... | collective-permute-start | bytes 49160 | tf_op jit(solution)/shard_map/ppermute | solution.py:318
  33.9 0.5 %collective-permute-start.11 = (f32[4,8,128]{2,1,0:T(8,128)S(1)}, f32[4,8,128]{2,1,0:T(8,128)S(1)}, u32[]{:S(2)}, u32[]{:S(2)}) collective-permute-start(f32[4,8,128]{2,1,0:T(8,128)S(1)} %get-tuple-element.32.mine), channel_id=1, source_target_pairs={{0,4},{2,6},{4,0},{6,2},{8,12},{10,14},{12,8},{14,10},{16,20},{18,... | collective-permute-start | bytes 49160 | tf_op jit(solution)/shard_map/ppermute | solution.py:318
  34.4 0.3 collective-permute-done.13.arrived
  34.7 1.8 %collective-permute-start.14 = (f32[4,8,128]{2,1,0:T(8,128)S(1)}, f32[4,8,128]{2,1,0:T(8,128)S(1)}, u32[]{:S(2)}, u32[]{:S(2)}) collective-permute-start(f32[4,8,128]{2,1,0:T(8,128)S(1)} %shard_map.53.mine), channel_id=1, source_target_pairs={{0,10},{2,8},{4,14},{6,12},{8,2},{10,0},{12,6},{14,4},{16,26},{18,... | collective-permute-start | bytes 49160 | tf_op jit(solution)/shard_map/ppermute | solution.py:318
  36.5 1.1 %collective-permute-done.11.arrived = f32[4,8,128]{2,1,0:T(8,128)S(1)} collective-permute-done((f32[4,8,128]{2,1,0:T(8,128)S(1)}, f32[4,8,128]{2,1,0:T(8,128)S(1)}, u32[]{:S(2)}, u32[]{:S(2)}) %collective-permute-start.11) | collective-permute-done | bytes 16416 | tf_op jit(solution)/shard_map/ppermute | solution.py:318
  37.6 0.6 %collective-permute-start.12 = (f32[4,8,128]{2,1,0:T(8,128)S(1)}, f32[4,8,128]{2,1,0:T(8,128)S(1)}, u32[]{:S(2)}, u32[]{:S(2)}) collective-permute-start(f32[4,8,128]{2,1,0:T(8,128)S(1)} %shard_map.52.rows_0_), channel_id=1, source_target_pairs={{0,1},{1,0},{2,3},{3,2},{4,5},{5,4},{6,7},{7,6},{8,9},{9,8},{10,11... | collective-permute-start | bytes 49160 | tf_op jit(solution)/shard_map/ppermute | solution.py:321
  38.2 3.1 %collective-permute-start.15 = (f32[4,8,128]{2,1,0:T(8,128)S(1)}, f32[4,8,128]{2,1,0:T(8,128)S(1)}, u32[]{:S(2)}, u32[]{:S(2)}) collective-permute-start(f32[4,8,128]{2,1,0:T(8,128)S(1)} %shard_map.54.cols_0_), channel_id=1, source_target_pairs={{0,18},{2,16},{4,22},{6,20},{8,26},{10,24},{12,30},{14,28},{16,2},... | collective-permute-start | bytes 49160 | tf_op jit(solution)/shard_map/ppermute | solution.py:318
  41.3 0.2 collective-permute-done.12.rows_1_
  41.4 1.3 %collective-permute-done.15.cols_1_ = f32[4,8,128]{2,1,0:T(8,128)S(1)} collective-permute-done((f32[4,8,128]{2,1,0:T(8,128)S(1)}, f32[4,8,128]{2,1,0:T(8,128)S(1)}, u32[]{:S(2)}, u32[]{:S(2)}) %collective-permute-start.15) | collective-permute-done | bytes 16416 | tf_op jit(solution)/shard_map/ppermute | solution.py:318
  42.7 1.5 %shard_map.55 = (f32[4,8,128]{2,1,0:T(8,128)S(1)}, f32[8,128]{1,0:T(8,128)S(1)}, f32[8,128]{1,0:T(8,128)S(1)}) custom-call(f32[768,512]{1,0:T(8,128)S(1)} %get-tuple-element.22.first, f32[768,512]{1,0:T(8,128)S(1)} %get-tuple-element.25.early_0_, f32[256,1024]{1,0:T(8,128)S(1)} %get-tuple-element.31.late, f32[4,8,128]{2,1,0:T(8,128)S(1)} %shard_map.52.rows_0_, ...), custom_call_target="tpu_custom_call" | custom-call | tf_op jit(solution)/shard_map/pallas_call | solution.py:267
  44.2 1.0 %collective-permute-start.16 = (f32[24,128]{1,0:T(8,128)S(1)}, f32[24,128]{1,0:T(8,128)S(1)}, u32[]{:S(2)}, u32[]{:S(2)}) collective-permute-start(f32[24,128]{1,0:T(8,128)S(1)} %pad_maximum_fusion), channel_id=1, source_target_pairs={{0,4},{2,6},{4,0},{6,2},{8,12},{10,14},{12,8},{14,10},{16,20},{18,... | collective-permute-start | bytes 36872 | tf_op jit(solution)/shard_map/ppermute | solution.py:318
  45.2 0.6 %slice_bitcast_fusion.2 = f32[512]{0:T(512)} fusion(f32[8,128]{1,0:T(8,128)S(1)} %get-tuple-element.34), kind=kLoop, calls=%fused_computation.5 | loop fusion | bytes 4096 | tf_op jit(solution)/shard_map/reshape | solution.py:428
  45.8 2.2 %collective-permute-done.16 = f32[24,128]{1,0:T(8,128)S(1)} collective-permute-done((f32[24,128]{1,0:T(8,128)S(1)}, f32[24,128]{1,0:T(8,128)S(1)}, u32[]{:S(2)}, u32[]{:S(2)}) %collective-permute-start.16) | collective-permute-done | bytes 12320 | tf_op jit(solution)/shard_map/ppermute | solution.py:318
  48.0 1.2 %collective-permute-start.17 = (f32[4,4,128]{2,1,0:T(4,128)S(1)}, f32[4,4,128]{2,1,0:T(4,128)S(1)}, u32[]{:S(2)}, u32[]{:S(2)}) collective-permute-start(f32[4,4,128]{2,1,0:T(4,128)S(1)} %shard_map.57.mine), channel_id=1, source_target_pairs={{0,1},{1,0},{2,3},{3,2},{4,5},{5,4},{6,7},{7,6},{8,9},{9,8},{10,11... | collective-permute-start | bytes 24584 | tf_op jit(solution)/shard_map/ppermute | solution.py:321
  49.2 0.6 %shard_map.56 = f32[16,128]{1,0:T(8,128)} custom-call(f32[16,128]{1,0:T(8,128)S(1)} %maximum_bitcast_fusion.known), custom_call_target="tpu_custom_call" | custom-call | tf_op jit(solution)/shard_map/pallas_call | solution.py:267
  49.8 1.9 %collective-permute-done.17.arrived = f32[4,4,128]{2,1,0:T(4,128)S(1)} collective-permute-done((f32[4,4,128]{2,1,0:T(4,128)S(1)}, f32[4,4,128]{2,1,0:T(4,128)S(1)}, u32[]{:S(2)}, u32[]{:S(2)}) %collective-permute-start.17) | collective-permute-done | bytes 8224 | tf_op jit(solution)/shard_map/ppermute | solution.py:321
  51.7 0.6 %copy.9 = f32[1,4,4,128]{3,1,2,0:T(4,128)} copy(f32[1,4,4,128]{3,2,1,0:T(4,128)S(1)} %bitcast.20) | data formatting | bytes 16384
  (28 shorter events, 0.2 us)
Async XLA Ops:
  0.6 19.6 %collective-permute-start = (bf16[512,512]{1,0:T(8,128)(2,1)}, bf16[512,512]{1,0:T(8,128)(2,1)S(1)}, u32[]{:S(2)}, u32[]{:S(2)}) collective-permute-start(bf16[512,512]{1,0:T(8,128)(2,1)} %source.1), channel_id=1, source_target_pairs={{0,1},{1,0},{2,3},{3,2},{4,5},{5,4},{6,7},{7,6},{8,9},{9,8},{10,11... | collective-permute-start | bytes 1572872 | tf_op jit(solution)/shard_map/ppermute | solution.py:325
  3.7 17.0 %collective-permute-start.6 = (bf16[512,512]{1,0:T(8,128)(2,1)}, bf16[512,512]{1,0:T(8,128)(2,1)S(1)}, u32[]{:S(2)}, u32[]{:S(2)}) collective-permute-start(bf16[512,512]{1,0:T(8,128)(2,1)} %source.1), channel_id=1, source_target_pairs={{0,4},{1,5},{2,6},{3,7},{4,0},{5,1},{6,2},{7,3},{8,12},{9,13},{10,... | collective-permute-start | bytes 1572872 | tf_op jit(solution)/shard_map/ppermute | solution.py:325
  5.2 14.3 %collective-permute-start.4 = (bf16[128,1024]{1,0:T(8,128)(2,1)}, bf16[128,1024]{1,0:T(8,128)(2,1)S(1)}, u32[]{:S(2)}, u32[]{:S(2)}) collective-permute-start(bf16[128,1024]{1,0:T(8,128)(2,1)} %target.1), channel_id=1, source_target_pairs={{0,16},{2,18},{4,20},{6,22},{8,24},{10,26},{12,28},{14,30},{16,0},... | collective-permute-start | bytes 786440 | tf_op jit(solution)/shard_map/ppermute | solution.py:318
  7.8 12.4 %collective-permute-start.2 = (bf16[128,1024]{1,0:T(8,128)(2,1)}, bf16[128,1024]{1,0:T(8,128)(2,1)S(1)}, u32[]{:S(2)}, u32[]{:S(2)}) collective-permute-start(bf16[128,1024]{1,0:T(8,128)(2,1)} %target.1), channel_id=1, source_target_pairs={{0,8},{2,10},{4,12},{6,14},{8,0},{10,2},{12,4},{14,6},{16,24},{18,... | collective-permute-start | bytes 786440 | tf_op jit(solution)/shard_map/ppermute | solution.py:318
  9.3 12.0 %collective-permute-start.1 = (bf16[128,1024]{1,0:T(8,128)(2,1)}, bf16[128,1024]{1,0:T(8,128)(2,1)S(1)}, u32[]{:S(2)}, u32[]{:S(2)}) collective-permute-start(bf16[128,1024]{1,0:T(8,128)(2,1)} %target.1), channel_id=1, source_target_pairs={{0,2},{2,0},{4,6},{6,4},{8,10},{10,8},{12,14},{14,12},{16,18},{18,... | collective-permute-start | bytes 786440 | tf_op jit(solution)/shard_map/ppermute | solution.py:318
  19.5 7.2 %collective-permute-start.9 = (bf16[128,1024]{1,0:T(8,128)(2,1)S(1)}, bf16[128,1024]{1,0:T(8,128)(2,1)S(1)}, u32[]{:S(2)}, u32[]{:S(2)}) collective-permute-start(bf16[128,1024]{1,0:T(8,128)(2,1)S(1)} %collective-permute-done.4.targets_4_), channel_id=1, source_target_pairs={{0,8},{2,10},{4,12},{6,14},{8,0},{10,2},{12,4},{14,6},{16,24},{18,... | collective-permute-start | bytes 786440 | tf_op jit(solution)/shard_map/ppermute | solution.py:318
  20.2 8.6 %collective-permute-start.5 = (bf16[128,1024]{1,0:T(8,128)(2,1)S(1)}, bf16[128,1024]{1,0:T(8,128)(2,1)S(1)}, u32[]{:S(2)}, u32[]{:S(2)}) collective-permute-start(bf16[128,1024]{1,0:T(8,128)(2,1)S(1)} %collective-permute-done.4.targets_4_), channel_id=1, source_target_pairs={{0,2},{2,0},{4,6},{6,4},{8,10},{10,8},{12,14},{14,12},{16,18},{18,... | collective-permute-start | bytes 786440 | tf_op jit(solution)/shard_map/ppermute | solution.py:318
  20.2 8.6 %collective-permute-start.3 = (bf16[128,1024]{1,0:T(8,128)(2,1)S(1)}, bf16[128,1024]{1,0:T(8,128)(2,1)S(1)}, u32[]{:S(2)}, u32[]{:S(2)}) collective-permute-start(bf16[128,1024]{1,0:T(8,128)(2,1)S(1)} %collective-permute-done.2.targets_2_), channel_id=1, source_target_pairs={{0,2},{2,0},{4,6},{6,4},{8,10},{10,8},{12,14},{14,12},{16,18},{18,... | collective-permute-start | bytes 786440 | tf_op jit(solution)/shard_map/ppermute | solution.py:318
  20.7 9.8 %collective-permute-start.7 = (bf16[256,512]{1,0:T(8,128)(2,1)S(1)}, bf16[256,512]{1,0:T(8,128)(2,1)S(1)}, u32[]{:S(2)}, u32[]{:S(2)}) collective-permute-start(bf16[256,512]{1,0:T(8,128)(2,1)S(1)} %slice.28), channel_id=1, source_target_pairs={{0,4},{2,6},{4,0},{6,2},{8,12},{10,14},{12,8},{14,10},{16,20},{18,... | collective-permute-start | bytes 786440 | tf_op jit(solution)/shard_map/ppermute | solution.py:318
  21.4 9.2 %collective-permute-start.8 = (bf16[256,512]{1,0:T(8,128)(2,1)S(1)}, bf16[256,512]{1,0:T(8,128)(2,1)S(1)}, u32[]{:S(2)}, u32[]{:S(2)}) collective-permute-start(bf16[256,512]{1,0:T(8,128)(2,1)S(1)} %slice.29), channel_id=1, source_target_pairs={{0,1},{1,0},{2,3},{3,2},{4,5},{5,4},{6,7},{7,6},{8,9},{9,8},{10,11... | collective-permute-start | bytes 786440 | tf_op jit(solution)/shard_map/ppermute | solution.py:321
  26.7 5.5 %collective-permute-start.10 = (bf16[128,1024]{1,0:T(8,128)(2,1)S(1)}, bf16[128,1024]{1,0:T(8,128)(2,1)S(1)}, u32[]{:S(2)}, u32[]{:S(2)}) collective-permute-start(bf16[128,1024]{1,0:T(8,128)(2,1)S(1)} %collective-permute-done.9.targets_0_), channel_id=1, source_target_pairs={{0,2},{2,0},{4,6},{6,4},{8,10},{10,8},{12,14},{14,12},{16,18},{18,... | collective-permute-start | bytes 786440 | tf_op jit(solution)/shard_map/ppermute | solution.py:318
  26.7 1.0 %copy-start = (bf16[512,512]{1,0:T(8,128)(2,1)S(1)}, bf16[512,512]{1,0:T(8,128)(2,1)}, u32[]{:S(2)}) copy-start(bf16[512,512]{1,0:T(8,128)(2,1)} %source.1) | copy-start | bytes 1572868
  27.7 0.9 %copy-start.1 = (bf16[128,1024]{1,0:T(8,128)(2,1)S(1)}, bf16[128,1024]{1,0:T(8,128)(2,1)}, u32[]{:S(2)}) copy-start(bf16[128,1024]{1,0:T(8,128)(2,1)} %target.1) | copy-start | bytes 786436
  33.3 1.4 %collective-permute-start.13 = (f32[4,8,128]{2,1,0:T(8,128)S(1)}, f32[4,8,128]{2,1,0:T(8,128)S(1)}, u32[]{:S(2)}, u32[]{:S(2)}) collective-permute-start(f32[4,8,128]{2,1,0:T(8,128)S(1)} %get-tuple-element.33.mine), channel_id=1, source_target_pairs={{0,2},{2,0},{4,6},{6,4},{8,10},{10,8},{12,14},{14,12},{16,18},{18,... | collective-permute-start | bytes 49160 | tf_op jit(solution)/shard_map/ppermute | solution.py:318
  33.9 3.7 %collective-permute-start.11 = (f32[4,8,128]{2,1,0:T(8,128)S(1)}, f32[4,8,128]{2,1,0:T(8,128)S(1)}, u32[]{:S(2)}, u32[]{:S(2)}) collective-permute-start(f32[4,8,128]{2,1,0:T(8,128)S(1)} %get-tuple-element.32.mine), channel_id=1, source_target_pairs={{0,4},{2,6},{4,0},{6,2},{8,12},{10,14},{12,8},{14,10},{16,20},{18,... | collective-permute-start | bytes 49160 | tf_op jit(solution)/shard_map/ppermute | solution.py:318
  34.7 3.5 %collective-permute-start.14 = (f32[4,8,128]{2,1,0:T(8,128)S(1)}, f32[4,8,128]{2,1,0:T(8,128)S(1)}, u32[]{:S(2)}, u32[]{:S(2)}) collective-permute-start(f32[4,8,128]{2,1,0:T(8,128)S(1)} %shard_map.53.mine), channel_id=1, source_target_pairs={{0,10},{2,8},{4,14},{6,12},{8,2},{10,0},{12,6},{14,4},{16,26},{18,... | collective-permute-start | bytes 49160 | tf_op jit(solution)/shard_map/ppermute | solution.py:318
  37.6 3.8 %collective-permute-start.12 = (f32[4,8,128]{2,1,0:T(8,128)S(1)}, f32[4,8,128]{2,1,0:T(8,128)S(1)}, u32[]{:S(2)}, u32[]{:S(2)}) collective-permute-start(f32[4,8,128]{2,1,0:T(8,128)S(1)} %shard_map.52.rows_0_), channel_id=1, source_target_pairs={{0,1},{1,0},{2,3},{3,2},{4,5},{5,4},{6,7},{7,6},{8,9},{9,8},{10,11... | collective-permute-start | bytes 49160 | tf_op jit(solution)/shard_map/ppermute | solution.py:321
  38.2 4.5 %collective-permute-start.15 = (f32[4,8,128]{2,1,0:T(8,128)S(1)}, f32[4,8,128]{2,1,0:T(8,128)S(1)}, u32[]{:S(2)}, u32[]{:S(2)}) collective-permute-start(f32[4,8,128]{2,1,0:T(8,128)S(1)} %shard_map.54.cols_0_), channel_id=1, source_target_pairs={{0,18},{2,16},{4,22},{6,20},{8,26},{10,24},{12,30},{14,28},{16,2},... | collective-permute-start | bytes 49160 | tf_op jit(solution)/shard_map/ppermute | solution.py:318
  44.2 3.8 %collective-permute-start.16 = (f32[24,128]{1,0:T(8,128)S(1)}, f32[24,128]{1,0:T(8,128)S(1)}, u32[]{:S(2)}, u32[]{:S(2)}) collective-permute-start(f32[24,128]{1,0:T(8,128)S(1)} %pad_maximum_fusion), channel_id=1, source_target_pairs={{0,4},{2,6},{4,0},{6,2},{8,12},{10,14},{12,8},{14,10},{16,20},{18,... | collective-permute-start | bytes 36872 | tf_op jit(solution)/shard_map/ppermute | solution.py:318
  48.0 3.7 %collective-permute-start.17 = (f32[4,4,128]{2,1,0:T(4,128)S(1)}, f32[4,4,128]{2,1,0:T(4,128)S(1)}, u32[]{:S(2)}, u32[]{:S(2)}) collective-permute-start(f32[4,4,128]{2,1,0:T(4,128)S(1)} %shard_map.57.mine), channel_id=1, source_target_pairs={{0,1},{1,0},{2,3},{3,2},{4,5},{5,4},{6,7},{7,6},{8,9},{9,8},{10,11... | collective-permute-start | bytes 24584 | tf_op jit(solution)/shard_map/ppermute | solution.py:321

commit v3 on v2

--- a/solution.py
+++ b/solution.py
@@ -209,32 +209,48 @@
         out_ref[k] = values
 
 
+def output_kernel(mine, arrived, out_ref, held, sem):
+    for k, values in enumerate(merged(mine, arrived, 0)):
+        for line in range(values.shape[0]):
+            held[k : k + 1, line * LANES : (line + 1) * LANES] = values[line : line + 1, :]
+    leaving = pltpu.make_async_copy(held, out_ref, sem)
+    leaving.start()
+    leaving.wait()
+
+
 def spread(ref, line):
     return jnp.broadcast_to(ref[line : line + 1, :] * 0.5, (LANES, LANES))
 
 
-def margin_kernel(unit, first, early, late, rows, cols, out_ref, fwd_ref, bwd_ref, bwd_down, held, sem):
-    n_early, slot = first.shape
-    n_late, n_src = late.shape
-    arriving = pltpu.make_async_copy(first, held, sem)
-    arriving.start()
-    early = [held, *early]
-    fwd_ref[...] = sum(merged(*rows, 0)) / K
-    bwd_ref[...] = sum(merged(*cols, unit)) / K
-    for t in range(0, n_early + n_late, LANES):
-        bwd_down[t : t + LANES, :] = spread(bwd_ref, t // LANES).T
-    for s in [*range(slot, n_src, LANES), *range(0, slot, LANES)]:
-        if s == 0:
-            arriving.wait()
-        fwd = spread(fwd_ref, s // LANES)
+def margin_lists(early, late, first, fwd_ref, bwd_down, out_ref):
+    n_early, n_late = early.shape[0], late.shape[0]
+    for s in range(0, early.shape[1], LANES):
+        fwd = spread(fwd_ref, (first + s) // LANES)
         lists = []
         for t in range(0, n_early + n_late, LANES):
             if t < n_early:
-                tile = early[s // slot][t : t + LANES, s % slot : s % slot + LANES]
+                tile = early[t : t + LANES, s : s + LANES]
             else:
-                tile = late[t - n_early : t - n_early + LANES, s : s + LANES]
+                tile = late[t - n_early : t - n_early + LANES, first + s : first + s + LANES]
             lists.append(fold(tile / (fwd + bwd_down[t : t + LANES, :])))
         store_lists(out_ref, fold_sublanes(reduce_lists(lists)), s // LANES)
+
+
+def sent_kernel(unit, early, late, rows, cols, *outs):
+    *lists, fwd_ref, bwd_ref, bwd_down = outs
+    fwd_ref[...] = sum(merged(*rows, 0)) / K
+    bwd_ref[...] = sum(merged(*cols, unit)) / K
+    for line in range(bwd_ref.shape[0]):
+        bwd_down[line * LANES : (line + 1) * LANES, :] = spread(bwd_ref, line).T
+    for n, out_ref in enumerate(lists):
+        margin_lists(early[n], late, (n + 1) * early[n].shape[1], fwd_ref, bwd_down, out_ref)
+
+
+def kept_kernel(first, late, fwd_ref, bwd_down, out_ref, held, sem):
+    arriving = pltpu.make_async_copy(first, held, sem)
+    arriving.start()
+    arriving.wait()
+    margin_lists(held, late, 0, fwd_ref, bwd_down, out_ref)
 
 
 def place_kernel(near, far, lines, known, out_ref):
@@ -393,46 +409,52 @@
             if 2 * bit < far:
                 col_best = merge_arrays(col_best, arrived, (2 * bit + 1) * t_rows)
         col_pair = [col_best, arrived]
-        margins, fwd, bwd = call(
-            functools.partial(margin_kernel, (far + 1) * t_rows),
-            (cosines[0], cosines[1:], cos_late, row_pair, col_pair),
-            [(K, src_lines, LANES), (src_lines, LANES), (tgt_lines, LANES)],
-            [(block_tgt, LANES), cosines[0].shape], hbm_in=(0,), sems=1,
+        lines = rows // LANES
+        *sent, fwd, bwd, bwd_down = call(
+            functools.partial(sent_kernel, (far + 1) * t_rows),
+            (cosines[1:], cos_late, row_pair, col_pair),
+            [(K, lines, LANES)] * (near - 1)
+            + [(src_lines, LANES), (tgt_lines, LANES), (block_tgt, LANES)],
         )
-        best = margins.reshape(K, near, rows // LANES, LANES)
+        (own,) = call(
+            kept_kernel, (cosines[0], cos_late, fwd, bwd_down),
+            [(K, lines, LANES)], [cosines[0].shape], 2 * block_tgt * rows * K, hbm_in=(0,), sems=1,
+        )
+        best = dict(enumerate([own, *sent]))
         known = bwd.reshape(1, tgt_lines, LANES)
-        kept = list(range(near))
         for bit in bits_below(near):
-            send = [n for n, slot in enumerate(kept) if slot & bit]
-            keep = [n for n, slot in enumerate(kept) if not slot & bit]
-            lists = jnp.concatenate([best[:, n : n + 1] for n in send], axis=1)
+            send = [slot for slot in best if slot & bit]
+            keep = [slot for slot in best if not slot & bit]
+            lists = jnp.concatenate([best[slot] for slot in send], axis=1)
             split = lists.size // LANES
             payload = jnp.concatenate(
                 [lists.reshape(split, LANES), known.reshape(-1, LANES)], axis=0
             )
             arrived = over_src(payload, 2 * bit)
-            mine = jnp.concatenate([best[:, n : n + 1] for n in keep], axis=1)
-            arrived_lists = arrived[:split].reshape(K, -1, LANES)
-            best = merge_arrays(mine.reshape(arrived_lists.shape), arrived_lists).reshape(mine.shape)
+            mine = jnp.concatenate([best[slot] for slot in keep], axis=1)
+            mine = merge_arrays(mine, arrived[:split].reshape(mine.shape))
+            best = {slot: mine[:, n * lines : (n + 1) * lines] for n, slot in enumerate(keep)}
             known = jnp.concatenate([known, arrived[split:].reshape(known.shape)], axis=0)
-            kept = [kept[n] for n in keep]
-        best = best.reshape(K, rows // LANES, LANES)
-        for bit in bits_below(n_tgt):
+        best = best[0]
+        for bit in bits_below(n_tgt)[:-1]:
             best = merge_arrays(best, over_tgt(best, bit))
+        (best,) = call(
+            output_kernel, (best, over_tgt(best, n_tgt // 2)),
+            [(K, rows)], [(K, rows)], hbm_out=(0,), sems=1,
+        )
         if t_rows % LANES == 0:
-            lines = t_rows // LANES
             (bwd_mean,) = call(
-                functools.partial(place_kernel, near, far, lines),
+                functools.partial(place_kernel, near, far, t_rows // LANES),
                 (known.reshape(-1, LANES),), [(near * tgt_lines, LANES)],
             )
-            return fwd[: rows // LANES].reshape(-1), bwd_mean.reshape(-1), best.reshape(K, rows)
+            return fwd[: rows // LANES].reshape(-1), bwd_mean.reshape(-1), best
         at = lax.axis_index("src")
         known = known.reshape(near, far, 2, t_rows)
         for axis, size, unit in ((0, near, 2), (1, far, 2 * near), (2, 2, 1)):
             for bit in bits_below(size):
                 known = flip_where(at & (unit * bit), known, axis, bit)
         bwd_mean = known.transpose(1, 0, 2, 3).reshape(-1)
-        return fwd[: rows // LANES].reshape(-1), bwd_mean, best.reshape(K, rows)
+        return fwd[: rows // LANES].reshape(-1), bwd_mean, best
 
     in_specs = (P("src", "tgt"), P(("tgt", "src"), None))
     out_specs = (P("src"), P("tgt"), P(None, "src"))

time: 52.5 us -> 51.8 us (0.987)
  waiting for transfers between devices: 21.8 us -> 21 us
  Pallas kernels: 6.71 us -> 7.36 us
  local copies, waits for them, and re-layouts: 3.22 us -> 2.61 us
    ppermute x13, waiting for transfers between devices: 19.7 us -> 19 us  [over_src(): return lax.ppermute(array, 'src', xor_pairs(n_src, mask))]
    pallas_call x10 -> x11, Pallas kernels: 6.64 us -> 7.28 us  [call(): pl.pallas_call(kernel, out_shape=tuple((jax.ShapeDtypeStruct(shape, jnp.f...]
    unnamed x5 -> x4, local copies, waits for them, and re-layouts: 2.6 us -> 1.99 us
  transfers between devices with their start and end apart: 18 -> 18, of which waited for: 8 -> 8; matrix products, arithmetic and copies ran while one was open for 1% -> 1% of each run, Pallas kernels for 8% -> 9%
where the time goes in v3:
time: 51.8 us; the launch traced here: 51.6 us
  waiting for transfers between devices  21 us (41%)
  starting transfers between devices  19.8 us (38%)
  Pallas kernels  7.36 us (14%)
  local copies, waits for them, and re-layouts  2.61 us (5%)
  between operations  0.76 us (1%)
    ppermute x13, waiting for transfers between devices, over_src(): return lax.ppermute(array, 'src', xor_pairs(n_src, mask))  19 us
    ppermute x13, starting transfers between devices, over_src(): return lax.ppermute(array, 'src', xor_pairs(n_src, mask))  12.9 us
    pallas_call x11, Pallas kernels, call(): pl.pallas_call(kernel, out_shape=tuple((jax.ShapeDtypeStruct(shape, jnp.f...  7.28 us
    ppermute x2, starting transfers between devices, over_both(): return lax.ppermute(array, ('src', 'tgt'), pairs)  4.55 us
    ppermute x3, starting transfers between devices, over_tgt(): return lax.ppermute(array, 'tgt', xor_pairs(n_tgt, mask))  2.34 us
    ppermute x3, waiting for transfers between devices, over_tgt(): return lax.ppermute(array, 'tgt', xor_pairs(n_tgt, mask))  2.04 us
    unnamed x4, local copies, waits for them, and re-layouts  1.99 us
  transfers between devices with their start and end apart: 18, of which 8 were waited for; matrix products, arithmetic and copies ran while one was open for 1% of the time, Pallas kernels for 9%

profile of v3, /device:TPU:0, one launch (start us, length us, event | category | flops | bytes accessed | tf_op | source)
XLA Modules:
  0.0 51.6 jit_solution(6623283586201905318)
XLA Ops:
  0.6 3.1 %collective-permute-start.1 = (bf16[512,512]{1,0:T(8,128)(2,1)}, bf16[512,512]{1,0:T(8,128)(2,1)S(1)}, u32[]{:S(2)}, u32[]{:S(2)}) collective-permute-start(bf16[512,512]{1,0:T(8,128)(2,1)} %source.1), channel_id=1, source_target_pairs={{0,1},{1,0},{2,3},{3,2},{4,5},{5,4},{6,7},{7,6},{8,9},{9,8},{10,11... | collective-permute-start | bytes 1572872 | tf_op jit(solution)/shard_map/ppermute | solution.py:341
  3.7 1.5 %collective-permute-start = (bf16[512,512]{1,0:T(8,128)(2,1)}, bf16[512,512]{1,0:T(8,128)(2,1)S(1)}, u32[]{:S(2)}, u32[]{:S(2)}) collective-permute-start(bf16[512,512]{1,0:T(8,128)(2,1)} %source.1), channel_id=1, source_target_pairs={{0,4},{1,5},{2,6},{3,7},{4,0},{5,1},{6,2},{7,3},{8,12},{9,13},{10,... | collective-permute-start | bytes 1572872 | tf_op jit(solution)/shard_map/ppermute | solution.py:341
  5.2 2.6 %collective-permute-start.7 = (bf16[128,1024]{1,0:T(8,128)(2,1)}, bf16[128,1024]{1,0:T(8,128)(2,1)S(1)}, u32[]{:S(2)}, u32[]{:S(2)}) collective-permute-start(bf16[128,1024]{1,0:T(8,128)(2,1)} %target.1), channel_id=1, source_target_pairs={{0,16},{2,18},{4,20},{6,22},{8,24},{10,26},{12,28},{14,30},{16,0},... | collective-permute-start | bytes 786440 | tf_op jit(solution)/shard_map/ppermute | solution.py:334
  7.8 1.6 %collective-permute-start.5 = (bf16[128,1024]{1,0:T(8,128)(2,1)}, bf16[128,1024]{1,0:T(8,128)(2,1)S(1)}, u32[]{:S(2)}, u32[]{:S(2)}) collective-permute-start(bf16[128,1024]{1,0:T(8,128)(2,1)} %target.1), channel_id=1, source_target_pairs={{0,8},{2,10},{4,12},{6,14},{8,0},{10,2},{12,4},{14,6},{16,24},{18,... | collective-permute-start | bytes 786440 | tf_op jit(solution)/shard_map/ppermute | solution.py:334
  9.4 10.1 %collective-permute-done.7.targets_4_ = bf16[128,1024]{1,0:T(8,128)(2,1)S(1)} collective-permute-done((bf16[128,1024]{1,0:T(8,128)(2,1)}, bf16[128,1024]{1,0:T(8,128)(2,1)S(1)}, u32[]{:S(2)}, u32[]{:S(2)}) %collective-permute-start.7) | collective-permute-done | bytes 262176 | tf_op jit(solution)/shard_map/ppermute | solution.py:334
  19.5 0.7 %collective-permute-start.9 = (bf16[128,1024]{1,0:T(8,128)(2,1)S(1)}, bf16[128,1024]{1,0:T(8,128)(2,1)S(1)}, u32[]{:S(2)}, u32[]{:S(2)}) collective-permute-start(bf16[128,1024]{1,0:T(8,128)(2,1)S(1)} %collective-permute-done.7.targets_4_), channel_id=1, source_target_pairs={{0,8},{2,10},{4,12},{6,14},{8,0},{10,2},{12,4},{14,6},{16,24},{18,... | collective-permute-start | bytes 786440 | tf_op jit(solution)/shard_map/ppermute | solution.py:334
  20.2 0.5 collective-permute-start.6
  20.7 0.6 %collective-permute-start.2 = (bf16[256,512]{1,0:T(8,128)(2,1)S(1)}, bf16[256,512]{1,0:T(8,128)(2,1)S(1)}, u32[]{:S(2)}, u32[]{:S(2)}) collective-permute-start(bf16[256,512]{1,0:T(8,128)(2,1)S(1)} %slice.20), channel_id=1, source_target_pairs={{0,4},{2,6},{4,0},{6,2},{8,12},{10,14},{12,8},{14,10},{16,20},{18,... | collective-permute-start | bytes 786440 | tf_op jit(solution)/shard_map/ppermute | solution.py:334
  21.4 0.6 %collective-permute-start.3 = (bf16[256,512]{1,0:T(8,128)(2,1)S(1)}, bf16[256,512]{1,0:T(8,128)(2,1)S(1)}, u32[]{:S(2)}, u32[]{:S(2)}) collective-permute-start(bf16[256,512]{1,0:T(8,128)(2,1)S(1)} %slice.21), channel_id=1, source_target_pairs={{0,1},{1,0},{2,3},{3,2},{4,5},{5,4},{6,7},{7,6},{8,9},{9,8},{10,11... | collective-permute-start | bytes 786440 | tf_op jit(solution)/shard_map/ppermute | solution.py:337
  21.9 4.7 %collective-permute-done.9.targets_0_ = bf16[128,1024]{1,0:T(8,128)(2,1)S(1)} collective-permute-done((bf16[128,1024]{1,0:T(8,128)(2,1)S(1)}, bf16[128,1024]{1,0:T(8,128)(2,1)S(1)}, u32[]{:S(2)}, u32[]{:S(2)}) %collective-permute-start.9) | collective-permute-done | bytes 262176 | tf_op jit(solution)/shard_map/ppermute | solution.py:334
  26.7 1.0 %copy-done = bf16[512,512]{1,0:T(8,128)(2,1)S(1)} copy-done((bf16[512,512]{1,0:T(8,128)(2,1)S(1)}, bf16[512,512]{1,0:T(8,128)(2,1)}, u32[]{:S(2)}) %copy-start) | copy-done | bytes 524312
  27.7 0.9 %copy-done.1 = bf16[128,1024]{1,0:T(8,128)(2,1)S(1)} copy-done((bf16[128,1024]{1,0:T(8,128)(2,1)S(1)}, bf16[128,1024]{1,0:T(8,128)(2,1)}, u32[]{:S(2)}) %copy-start.1) | copy-done | bytes 262168
  28.8 1.8 %shard_map.49 = (f32[768,512]{1,0:T(8,128)S(1)}, f32[8,512]{1,0:T(8,128)S(1)}, f32[768,128]{1,0:T(8,128)S(1)}, f32[4,8,512]{2,1,0:T(8,128)S(1)}, f32[4,8,768]{2,1,0:T(8,128)S(1)}) custom-call(bf16[512,512]{1,0:T(8,128)(2,1)S(1)} %get-tuple-element.22.piece_0__0_.pieces_0__0__0_, bf16[512,512]{1,0:T(8,128)(2,1)S(1)} %collective-permute-done.1.piece_1__0_.pieces_0__1__0_, ...), custom_call_target="tpu_custom_call" | custom-call | flops 805306368 | tf_op jit(solution)/shard_map/pallas_call | solution.py:283
  30.5 1.6 %shard_map.50 = (f32[768,512]{1,0:T(8,128)S(1)}, f32[8,512]{1,0:T(8,128)S(1)}, f32[4,8,512]{2,1,0:T(8,128)S(1)}, f32[4,8,768]{2,1,0:T(8,128)S(1)}) custom-call(bf16[512,512]{1,0:T(8,128)(2,1)S(1)} %collective-permute-done.piece_0__0_.pieces_1__0__0_, bf16[256,512]{1,0:T(8,128)(2,1)S(1)} %collective-permute-done.2.piece_1__0_.pieces_1__1__0_, ...), custom_call_target="tpu_custom_call" | custom-call | flops 805306368 | tf_op jit(solution)/shard_map/pallas_call | solution.py:283
  32.2 1.1 %shard_map.51 = (f32[256,1024]{1,0:T(8,128)S(1)}, f32[4,8,128]{2,1,0:T(8,128)S(1)}, f32[4,8,128]{2,1,0:T(8,128)S(1)}) custom-call(bf16[512,512]{1,0:T(8,128)(2,1)S(1)} %get-tuple-element.22.piece_0__0_.pieces_0__0__0_, bf16[512,512]{1,0:T(8,128)(2,1)S(1)} %collective-permute-done.1.piece_1__0_.pieces_0__1__0_, ...), custom_call_target="tpu_custom_call" | custom-call | flops 536870912 | tf_op jit(solution)/shard_map/pallas_call | solution.py:283
  33.3 0.6 %collective-permute-start.13 = (f32[4,8,128]{2,1,0:T(8,128)S(1)}, f32[4,8,128]{2,1,0:T(8,128)S(1)}, u32[]{:S(2)}, u32[]{:S(2)}) collective-permute-start(f32[4,8,128]{2,1,0:T(8,128)S(1)} %get-tuple-element.33.mine), channel_id=1, source_target_pairs={{0,2},{2,0},{4,6},{6,4},{8,10},{10,8},{12,14},{14,12},{16,18},{18,... | collective-permute-start | bytes 49160 | tf_op jit(solution)/shard_map/ppermute | solution.py:334
  33.9 0.5 %collective-permute-start.11 = (f32[4,8,128]{2,1,0:T(8,128)S(1)}, f32[4,8,128]{2,1,0:T(8,128)S(1)}, u32[]{:S(2)}, u32[]{:S(2)}) collective-permute-start(f32[4,8,128]{2,1,0:T(8,128)S(1)} %get-tuple-element.32.mine), channel_id=1, source_target_pairs={{0,4},{2,6},{4,0},{6,2},{8,12},{10,14},{12,8},{14,10},{16,20},{18,... | collective-permute-start | bytes 49160 | tf_op jit(solution)/shard_map/ppermute | solution.py:334
  34.4 0.3 collective-permute-done.13.arrived
  34.7 1.8 %collective-permute-start.14 = (f32[4,8,128]{2,1,0:T(8,128)S(1)}, f32[4,8,128]{2,1,0:T(8,128)S(1)}, u32[]{:S(2)}, u32[]{:S(2)}) collective-permute-start(f32[4,8,128]{2,1,0:T(8,128)S(1)} %shard_map.53.mine), channel_id=1, source_target_pairs={{0,10},{2,8},{4,14},{6,12},{8,2},{10,0},{12,6},{14,4},{16,26},{18,... | collective-permute-start | bytes 49160 | tf_op jit(solution)/shard_map/ppermute | solution.py:334
  36.5 1.1 %collective-permute-done.11.arrived = f32[4,8,128]{2,1,0:T(8,128)S(1)} collective-permute-done((f32[4,8,128]{2,1,0:T(8,128)S(1)}, f32[4,8,128]{2,1,0:T(8,128)S(1)}, u32[]{:S(2)}, u32[]{:S(2)}) %collective-permute-start.11) | collective-permute-done | bytes 16416 | tf_op jit(solution)/shard_map/ppermute | solution.py:334
  37.6 0.6 %collective-permute-start.12 = (f32[4,8,128]{2,1,0:T(8,128)S(1)}, f32[4,8,128]{2,1,0:T(8,128)S(1)}, u32[]{:S(2)}, u32[]{:S(2)}) collective-permute-start(f32[4,8,128]{2,1,0:T(8,128)S(1)} %shard_map.52.rows_0_), channel_id=1, source_target_pairs={{0,1},{1,0},{2,3},{3,2},{4,5},{5,4},{6,7},{7,6},{8,9},{9,8},{10,11... | collective-permute-start | bytes 49160 | tf_op jit(solution)/shard_map/ppermute | solution.py:337
  38.2 3.1 %collective-permute-start.15 = (f32[4,8,128]{2,1,0:T(8,128)S(1)}, f32[4,8,128]{2,1,0:T(8,128)S(1)}, u32[]{:S(2)}, u32[]{:S(2)}) collective-permute-start(f32[4,8,128]{2,1,0:T(8,128)S(1)} %shard_map.54.cols_0_), channel_id=1, source_target_pairs={{0,18},{2,16},{4,22},{6,20},{8,26},{10,24},{12,30},{14,28},{16,2},... | collective-permute-start | bytes 49160 | tf_op jit(solution)/shard_map/ppermute | solution.py:334
  41.4 1.3 %collective-permute-done.15.cols_1_ = f32[4,8,128]{2,1,0:T(8,128)S(1)} collective-permute-done((f32[4,8,128]{2,1,0:T(8,128)S(1)}, f32[4,8,128]{2,1,0:T(8,128)S(1)}, u32[]{:S(2)}, u32[]{:S(2)}) %collective-permute-start.15) | collective-permute-done | bytes 16416 | tf_op jit(solution)/shard_map/ppermute | solution.py:334
  42.7 0.8 %shard_map.55 = (f32[4,4,128]{2,1,0:T(4,128)S(1)}, f32[8,128]{1,0:T(8,128)S(1)}, f32[8,128]{1,0:T(8,128)S(1)}, f32[1024,128]{1,0:T(8,128)S(1)}) custom-call(f32[768,512]{1,0:T(8,128)S(1)} %get-tuple-element.25.early_0_, f32[256,1024]{1,0:T(8,128)S(1)} %get-tuple-element.31.late, f32[4,8,128]{2,1,0:T(8,128)S(1)} %shard_map.52.rows_0_, ...), custom_call_target="tpu_custom_call" | custom-call | tf_op jit(solution)/shard_map/pallas_call | solution.py:283
  43.5 1.0 %collective-permute-start.16 = (f32[24,128]{1,0:T(8,128)S(1)}, f32[24,128]{1,0:T(8,128)S(1)}, u32[]{:S(2)}, u32[]{:S(2)}) collective-permute-start(f32[24,128]{1,0:T(8,128)S(1)} %pad_maximum_fusion), channel_id=1, source_target_pairs={{0,4},{2,6},{4,0},{6,2},{8,12},{10,14},{12,8},{14,10},{16,20},{18,... | collective-permute-start | bytes 36872 | tf_op jit(solution)/shard_map/ppermute | solution.py:334
  44.5 0.6 %slice_bitcast_fusion.1 = f32[512]{0:T(512)} fusion(f32[8,128]{1,0:T(8,128)S(1)} %get-tuple-element.34.fwd_ref), kind=kLoop, calls=%fused_computation.3 | loop fusion | bytes 4096 | tf_op jit(solution)/shard_map/reshape | solution.py:450
  45.1 0.7 %shard_map.57.mine = f32[4,4,128]{2,1,0:T(4,128)S(1)} custom-call(f32[768,512]{1,0:T(8,128)S(1)} %get-tuple-element.37.first, f32[256,1024]{1,0:T(8,128)S(1)} %get-tuple-element.31.late, f32[8,128]{1,0:T(8,128)S(1)} %get-tuple-element.34.fwd_ref, f32[1024,128]{1,0:T(8,128)S(1)} %get-tuple-element.38.bwd_down), custom_call_target="tpu_custom_call" | custom-call | flops 4194304 | tf_op jit(solution)/shard_map/pallas_call | solution.py:283
  45.8 1.4 %collective-permute-done.16 = f32[24,128]{1,0:T(8,128)S(1)} collective-permute-done((f32[24,128]{1,0:T(8,128)S(1)}, f32[24,128]{1,0:T(8,128)S(1)}, u32[]{:S(2)}, u32[]{:S(2)}) %collective-permute-start.16) | collective-permute-done | bytes 12320 | tf_op jit(solution)/shard_map/ppermute | solution.py:334
  47.3 1.2 %collective-permute-start.17 = (f32[4,4,128]{2,1,0:T(4,128)S(1)}, f32[4,4,128]{2,1,0:T(4,128)S(1)}, u32[]{:S(2)}, u32[]{:S(2)}) collective-permute-start(f32[4,4,128]{2,1,0:T(4,128)S(1)} %shard_map.58.mine), channel_id=1, source_target_pairs={{0,1},{1,0},{2,3},{3,2},{4,5},{5,4},{6,7},{7,6},{8,9},{9,8},{10,11... | collective-permute-start | bytes 24584 | tf_op jit(solution)/shard_map/ppermute | solution.py:337
  48.5 0.6 %shard_map.56 = f32[16,128]{1,0:T(8,128)} custom-call(f32[16,128]{1,0:T(8,128)S(1)} %maximum_bitcast_fusion.known), custom_call_target="tpu_custom_call" | custom-call | tf_op jit(solution)/shard_map/pallas_call | solution.py:283
  49.1 1.9 %collective-permute-done.17.arrived = f32[4,4,128]{2,1,0:T(4,128)S(1)} collective-permute-done((f32[4,4,128]{2,1,0:T(4,128)S(1)}, f32[4,4,128]{2,1,0:T(4,128)S(1)}, u32[]{:S(2)}, u32[]{:S(2)}) %collective-permute-start.17) | collective-permute-done | bytes 8224 | tf_op jit(solution)/shard_map/ppermute | solution.py:337
  51.0 0.6 %shard_map.59 = f32[4,512]{1,0:T(4,128)} custom-call(f32[4,4,128]{2,1,0:T(4,128)S(1)} %shard_map.58.mine, f32[4,4,128]{2,1,0:T(4,128)S(1)} %collective-permute-done.17.arrived), custom_call_target="tpu_custom_call" | custom-call | tf_op jit(solution)/shard_map/pallas_call | solution.py:283
  (27 shorter events, 0.4 us)
Async XLA Ops:
  0.6 19.6 %collective-permute-start.1 = (bf16[512,512]{1,0:T(8,128)(2,1)}, bf16[512,512]{1,0:T(8,128)(2,1)S(1)}, u32[]{:S(2)}, u32[]{:S(2)}) collective-permute-start(bf16[512,512]{1,0:T(8,128)(2,1)} %source.1), channel_id=1, source_target_pairs={{0,1},{1,0},{2,3},{3,2},{4,5},{5,4},{6,7},{7,6},{8,9},{9,8},{10,11... | collective-permute-start | bytes 1572872 | tf_op jit(solution)/shard_map/ppermute | solution.py:341
  3.7 17.0 %collective-permute-start = (bf16[512,512]{1,0:T(8,128)(2,1)}, bf16[512,512]{1,0:T(8,128)(2,1)S(1)}, u32[]{:S(2)}, u32[]{:S(2)}) collective-permute-start(bf16[512,512]{1,0:T(8,128)(2,1)} %source.1), channel_id=1, source_target_pairs={{0,4},{1,5},{2,6},{3,7},{4,0},{5,1},{6,2},{7,3},{8,12},{9,13},{10,... | collective-permute-start | bytes 1572872 | tf_op jit(solution)/shard_map/ppermute | solution.py:341
  5.2 14.3 %collective-permute-start.7 = (bf16[128,1024]{1,0:T(8,128)(2,1)}, bf16[128,1024]{1,0:T(8,128)(2,1)S(1)}, u32[]{:S(2)}, u32[]{:S(2)}) collective-permute-start(bf16[128,1024]{1,0:T(8,128)(2,1)} %target.1), channel_id=1, source_target_pairs={{0,16},{2,18},{4,20},{6,22},{8,24},{10,26},{12,28},{14,30},{16,0},... | collective-permute-start | bytes 786440 | tf_op jit(solution)/shard_map/ppermute | solution.py:334
  7.8 12.4 %collective-permute-start.5 = (bf16[128,1024]{1,0:T(8,128)(2,1)}, bf16[128,1024]{1,0:T(8,128)(2,1)S(1)}, u32[]{:S(2)}, u32[]{:S(2)}) collective-permute-start(bf16[128,1024]{1,0:T(8,128)(2,1)} %target.1), channel_id=1, source_target_pairs={{0,8},{2,10},{4,12},{6,14},{8,0},{10,2},{12,4},{14,6},{16,24},{18,... | collective-permute-start | bytes 786440 | tf_op jit(solution)/shard_map/ppermute | solution.py:334
  9.3 12.0 %collective-permute-start.4 = (bf16[128,1024]{1,0:T(8,128)(2,1)}, bf16[128,1024]{1,0:T(8,128)(2,1)S(1)}, u32[]{:S(2)}, u32[]{:S(2)}) collective-permute-start(bf16[128,1024]{1,0:T(8,128)(2,1)} %target.1), channel_id=1, source_target_pairs={{0,2},{2,0},{4,6},{6,4},{8,10},{10,8},{12,14},{14,12},{16,18},{18,... | collective-permute-start | bytes 786440 | tf_op jit(solution)/shard_map/ppermute | solution.py:334
  19.5 7.2 %collective-permute-start.9 = (bf16[128,1024]{1,0:T(8,128)(2,1)S(1)}, bf16[128,1024]{1,0:T(8,128)(2,1)S(1)}, u32[]{:S(2)}, u32[]{:S(2)}) collective-permute-start(bf16[128,1024]{1,0:T(8,128)(2,1)S(1)} %collective-permute-done.7.targets_4_), channel_id=1, source_target_pairs={{0,8},{2,10},{4,12},{6,14},{8,0},{10,2},{12,4},{14,6},{16,24},{18,... | collective-permute-start | bytes 786440 | tf_op jit(solution)/shard_map/ppermute | solution.py:334
  20.2 8.6 %collective-permute-start.8 = (bf16[128,1024]{1,0:T(8,128)(2,1)S(1)}, bf16[128,1024]{1,0:T(8,128)(2,1)S(1)}, u32[]{:S(2)}, u32[]{:S(2)}) collective-permute-start(bf16[128,1024]{1,0:T(8,128)(2,1)S(1)} %collective-permute-done.7.targets_4_), channel_id=1, source_target_pairs={{0,2},{2,0},{4,6},{6,4},{8,10},{10,8},{12,14},{14,12},{16,18},{18,... | collective-permute-start | bytes 786440 | tf_op jit(solution)/shard_map/ppermute | solution.py:334
  20.2 8.6 %collective-permute-start.6 = (bf16[128,1024]{1,0:T(8,128)(2,1)S(1)}, bf16[128,1024]{1,0:T(8,128)(2,1)S(1)}, u32[]{:S(2)}, u32[]{:S(2)}) collective-permute-start(bf16[128,1024]{1,0:T(8,128)(2,1)S(1)} %collective-permute-done.5.targets_2_), channel_id=1, source_target_pairs={{0,2},{2,0},{4,6},{6,4},{8,10},{10,8},{12,14},{14,12},{16,18},{18,... | collective-permute-start | bytes 786440 | tf_op jit(solution)/shard_map/ppermute | solution.py:334
  20.7 9.8 %collective-permute-start.2 = (bf16[256,512]{1,0:T(8,128)(2,1)S(1)}, bf16[256,512]{1,0:T(8,128)(2,1)S(1)}, u32[]{:S(2)}, u32[]{:S(2)}) collective-permute-start(bf16[256,512]{1,0:T(8,128)(2,1)S(1)} %slice.20), channel_id=1, source_target_pairs={{0,4},{2,6},{4,0},{6,2},{8,12},{10,14},{12,8},{14,10},{16,20},{18,... | collective-permute-start | bytes 786440 | tf_op jit(solution)/shard_map/ppermute | solution.py:334
  21.4 9.2 %collective-permute-start.3 = (bf16[256,512]{1,0:T(8,128)(2,1)S(1)}, bf16[256,512]{1,0:T(8,128)(2,1)S(1)}, u32[]{:S(2)}, u32[]{:S(2)}) collective-permute-start(bf16[256,512]{1,0:T(8,128)(2,1)S(1)} %slice.21), channel_id=1, source_target_pairs={{0,1},{1,0},{2,3},{3,2},{4,5},{5,4},{6,7},{7,6},{8,9},{9,8},{10,11... | collective-permute-start | bytes 786440 | tf_op jit(solution)/shard_map/ppermute | solution.py:337
  26.7 5.5 %collective-permute-start.10 = (bf16[128,1024]{1,0:T(8,128)(2,1)S(1)}, bf16[128,1024]{1,0:T(8,128)(2,1)S(1)}, u32[]{:S(2)}, u32[]{:S(2)}) collective-permute-start(bf16[128,1024]{1,0:T(8,128)(2,1)S(1)} %collective-permute-done.9.targets_0_), channel_id=1, source_target_pairs={{0,2},{2,0},{4,6},{6,4},{8,10},{10,8},{12,14},{14,12},{16,18},{18,... | collective-permute-start | bytes 786440 | tf_op jit(solution)/shard_map/ppermute | solution.py:334
  26.7 1.0 %copy-start = (bf16[512,512]{1,0:T(8,128)(2,1)S(1)}, bf16[512,512]{1,0:T(8,128)(2,1)}, u32[]{:S(2)}) copy-start(bf16[512,512]{1,0:T(8,128)(2,1)} %source.1) | copy-start | bytes 1572868
  27.7 0.9 %copy-start.1 = (bf16[128,1024]{1,0:T(8,128)(2,1)S(1)}, bf16[128,1024]{1,0:T(8,128)(2,1)}, u32[]{:S(2)}) copy-start(bf16[128,1024]{1,0:T(8,128)(2,1)} %target.1) | copy-start | bytes 786436
  33.3 1.4 %collective-permute-start.13 = (f32[4,8,128]{2,1,0:T(8,128)S(1)}, f32[4,8,128]{2,1,0:T(8,128)S(1)}, u32[]{:S(2)}, u32[]{:S(2)}) collective-permute-start(f32[4,8,128]{2,1,0:T(8,128)S(1)} %get-tuple-element.33.mine), channel_id=1, source_target_pairs={{0,2},{2,0},{4,6},{6,4},{8,10},{10,8},{12,14},{14,12},{16,18},{18,... | collective-permute-start | bytes 49160 | tf_op jit(solution)/shard_map/ppermute | solution.py:334
  33.9 3.7 %collective-permute-start.11 = (f32[4,8,128]{2,1,0:T(8,128)S(1)}, f32[4,8,128]{2,1,0:T(8,128)S(1)}, u32[]{:S(2)}, u32[]{:S(2)}) collective-permute-start(f32[4,8,128]{2,1,0:T(8,128)S(1)} %get-tuple-element.32.mine), channel_id=1, source_target_pairs={{0,4},{2,6},{4,0},{6,2},{8,12},{10,14},{12,8},{14,10},{16,20},{18,... | collective-permute-start | bytes 49160 | tf_op jit(solution)/shard_map/ppermute | solution.py:334
  34.7 3.5 %collective-permute-start.14 = (f32[4,8,128]{2,1,0:T(8,128)S(1)}, f32[4,8,128]{2,1,0:T(8,128)S(1)}, u32[]{:S(2)}, u32[]{:S(2)}) collective-permute-start(f32[4,8,128]{2,1,0:T(8,128)S(1)} %shard_map.53.mine), channel_id=1, source_target_pairs={{0,10},{2,8},{4,14},{6,12},{8,2},{10,0},{12,6},{14,4},{16,26},{18,... | collective-permute-start | bytes 49160 | tf_op jit(solution)/shard_map/ppermute | solution.py:334
  37.6 3.8 %collective-permute-start.12 = (f32[4,8,128]{2,1,0:T(8,128)S(1)}, f32[4,8,128]{2,1,0:T(8,128)S(1)}, u32[]{:S(2)}, u32[]{:S(2)}) collective-permute-start(f32[4,8,128]{2,1,0:T(8,128)S(1)} %shard_map.52.rows_0_), channel_id=1, source_target_pairs={{0,1},{1,0},{2,3},{3,2},{4,5},{5,4},{6,7},{7,6},{8,9},{9,8},{10,11... | collective-permute-start | bytes 49160 | tf_op jit(solution)/shard_map/ppermute | solution.py:337
  38.2 4.5 %collective-permute-start.15 = (f32[4,8,128]{2,1,0:T(8,128)S(1)}, f32[4,8,128]{2,1,0:T(8,128)S(1)}, u32[]{:S(2)}, u32[]{:S(2)}) collective-permute-start(f32[4,8,128]{2,1,0:T(8,128)S(1)} %shard_map.54.cols_0_), channel_id=1, source_target_pairs={{0,18},{2,16},{4,22},{6,20},{8,26},{10,24},{12,30},{14,28},{16,2},... | collective-permute-start | bytes 49160 | tf_op jit(solution)/shard_map/ppermute | solution.py:334
  43.5 3.8 %collective-permute-start.16 = (f32[24,128]{1,0:T(8,128)S(1)}, f32[24,128]{1,0:T(8,128)S(1)}, u32[]{:S(2)}, u32[]{:S(2)}) collective-permute-start(f32[24,128]{1,0:T(8,128)S(1)} %pad_maximum_fusion), channel_id=1, source_target_pairs={{0,4},{2,6},{4,0},{6,2},{8,12},{10,14},{12,8},{14,10},{16,20},{18,... | collective-permute-start | bytes 36872 | tf_op jit(solution)/shard_map/ppermute | solution.py:334
  47.3 3.7 %collective-permute-start.17 = (f32[4,4,128]{2,1,0:T(4,128)S(1)}, f32[4,4,128]{2,1,0:T(4,128)S(1)}, u32[]{:S(2)}, u32[]{:S(2)}) collective-permute-start(f32[4,4,128]{2,1,0:T(4,128)S(1)} %shard_map.58.mine), channel_id=1, source_target_pairs={{0,1},{1,0},{2,3},{3,2},{4,5},{5,4},{6,7},{7,6},{8,9},{9,8},{10,11... | collective-permute-start | bytes 24584 | tf_op jit(solution)/shard_map/ppermute | solution.py:337

commit v4 on v3

--- a/solution.py
+++ b/solution.py
@@ -207,15 +207,6 @@
 def merge_kernel(unit, mine, arrived, out_ref):
     for k, values in enumerate(merged(mine, arrived, unit)):
         out_ref[k] = values
-
-
-def output_kernel(mine, arrived, out_ref, held, sem):
-    for k, values in enumerate(merged(mine, arrived, 0)):
-        for line in range(values.shape[0]):
-            held[k : k + 1, line * LANES : (line + 1) * LANES] = values[line : line + 1, :]
-    leaving = pltpu.make_async_copy(held, out_ref, sem)
-    leaving.start()
-    leaving.wait()
 
 
 def spread(ref, line):
@@ -436,25 +427,21 @@
             best = {slot: mine[:, n * lines : (n + 1) * lines] for n, slot in enumerate(keep)}
             known = jnp.concatenate([known, arrived[split:].reshape(known.shape)], axis=0)
         best = best[0]
-        for bit in bits_below(n_tgt)[:-1]:
+        for bit in bits_below(n_tgt):
             best = merge_arrays(best, over_tgt(best, bit))
-        (best,) = call(
-            output_kernel, (best, over_tgt(best, n_tgt // 2)),
-            [(K, rows)], [(K, rows)], hbm_out=(0,), sems=1,
-        )
         if t_rows % LANES == 0:
             (bwd_mean,) = call(
                 functools.partial(place_kernel, near, far, t_rows // LANES),
                 (known.reshape(-1, LANES),), [(near * tgt_lines, LANES)],
             )
-            return fwd[: rows // LANES].reshape(-1), bwd_mean.reshape(-1), best
+            return fwd[: rows // LANES].reshape(-1), bwd_mean.reshape(-1), best.reshape(K, rows)
         at = lax.axis_index("src")
         known = known.reshape(near, far, 2, t_rows)
         for axis, size, unit in ((0, near, 2), (1, far, 2 * near), (2, 2, 1)):
             for bit in bits_below(size):
                 known = flip_where(at & (unit * bit), known, axis, bit)
         bwd_mean = known.transpose(1, 0, 2, 3).reshape(-1)
-        return fwd[: rows // LANES].reshape(-1), bwd_mean, best
+        return fwd[: rows // LANES].reshape(-1), bwd_mean, best.reshape(K, rows)
 
     in_specs = (P("src", "tgt"), P(("tgt", "src"), None))
     out_specs = (P("src"), P("tgt"), P(None, "src"))

time: 51.8 us -> 51.8 us (level)
  Pallas kernels: 7.36 us -> 6.75 us
  local copies, waits for them, and re-layouts: 2.61 us -> 3.21 us
    pallas_call x11, Pallas kernels: 7.28 us -> 6.68 us  [call(): pl.pallas_call(kernel, out_shape=tuple((jax.ShapeDtypeStruct(shape, jnp.f...]
    unnamed x4 -> x5, local copies, waits for them, and re-layouts: 1.99 us -> 2.6 us
where the time goes in v4:
time: 51.8 us; the launch traced here: 51.6 us
  waiting for transfers between devices  21 us (41%)
  starting transfers between devices  19.8 us (38%)
  Pallas kernels  6.75 us (13%)
  local copies, waits for them, and re-layouts  3.21 us (6%)
  between operations  0.76 us (1%)
    ppermute x13, waiting for transfers between devices, over_src(): return lax.ppermute(array, 'src', xor_pairs(n_src, mask))  19 us
    ppermute x13, starting transfers between devices, over_src(): return lax.ppermute(array, 'src', xor_pairs(n_src, mask))  12.9 us
    pallas_call x11, Pallas kernels, call(): pl.pallas_call(kernel, out_shape=tuple((jax.ShapeDtypeStruct(shape, jnp.f...  6.68 us
    ppermute x2, starting transfers between devices, over_both(): return lax.ppermute(array, ('src', 'tgt'), pairs)  4.55 us
    unnamed x5, local copies, waits for them, and re-layouts  2.6 us
    ppermute x3, starting transfers between devices, over_tgt(): return lax.ppermute(array, 'tgt', xor_pairs(n_tgt, mask))  2.34 us
    ppermute x3, waiting for transfers between devices, over_tgt(): return lax.ppermute(array, 'tgt', xor_pairs(n_tgt, mask))  2.04 us
  transfers between devices with their start and end apart: 18, of which 8 were waited for; matrix products, arithmetic and copies ran while one was open for 1% of the time, Pallas kernels for 9%

profile of v4, /device:TPU:0, one launch (start us, length us, event | category | flops | bytes accessed | tf_op | source)
XLA Modules:
  0.0 51.6 jit_solution(14003850744400715811)
XLA Ops:
  0.6 3.1 %collective-permute-start.1 = (bf16[512,512]{1,0:T(8,128)(2,1)}, bf16[512,512]{1,0:T(8,128)(2,1)S(1)}, u32[]{:S(2)}, u32[]{:S(2)}) collective-permute-start(bf16[512,512]{1,0:T(8,128)(2,1)} %source.1), channel_id=1, source_target_pairs={{0,1},{1,0},{2,3},{3,2},{4,5},{5,4},{6,7},{7,6},{8,9},{9,8},{10,11... | collective-permute-start | bytes 1572872 | tf_op jit(solution)/shard_map/ppermute | solution.py:332
  3.7 1.5 %collective-permute-start = (bf16[512,512]{1,0:T(8,128)(2,1)}, bf16[512,512]{1,0:T(8,128)(2,1)S(1)}, u32[]{:S(2)}, u32[]{:S(2)}) collective-permute-start(bf16[512,512]{1,0:T(8,128)(2,1)} %source.1), channel_id=1, source_target_pairs={{0,4},{1,5},{2,6},{3,7},{4,0},{5,1},{6,2},{7,3},{8,12},{9,13},{10,... | collective-permute-start | bytes 1572872 | tf_op jit(solution)/shard_map/ppermute | solution.py:332
  5.2 2.6 %collective-permute-start.7 = (bf16[128,1024]{1,0:T(8,128)(2,1)}, bf16[128,1024]{1,0:T(8,128)(2,1)S(1)}, u32[]{:S(2)}, u32[]{:S(2)}) collective-permute-start(bf16[128,1024]{1,0:T(8,128)(2,1)} %target.1), channel_id=1, source_target_pairs={{0,16},{2,18},{4,20},{6,22},{8,24},{10,26},{12,28},{14,30},{16,0},... | collective-permute-start | bytes 786440 | tf_op jit(solution)/shard_map/ppermute | solution.py:325
  7.8 1.6 %collective-permute-start.5 = (bf16[128,1024]{1,0:T(8,128)(2,1)}, bf16[128,1024]{1,0:T(8,128)(2,1)S(1)}, u32[]{:S(2)}, u32[]{:S(2)}) collective-permute-start(bf16[128,1024]{1,0:T(8,128)(2,1)} %target.1), channel_id=1, source_target_pairs={{0,8},{2,10},{4,12},{6,14},{8,0},{10,2},{12,4},{14,6},{16,24},{18,... | collective-permute-start | bytes 786440 | tf_op jit(solution)/shard_map/ppermute | solution.py:325
  9.4 10.1 %collective-permute-done.7.targets_4_ = bf16[128,1024]{1,0:T(8,128)(2,1)S(1)} collective-permute-done((bf16[128,1024]{1,0:T(8,128)(2,1)}, bf16[128,1024]{1,0:T(8,128)(2,1)S(1)}, u32[]{:S(2)}, u32[]{:S(2)}) %collective-permute-start.7) | collective-permute-done | bytes 262176 | tf_op jit(solution)/shard_map/ppermute | solution.py:325
  19.5 0.7 %collective-permute-start.9 = (bf16[128,1024]{1,0:T(8,128)(2,1)S(1)}, bf16[128,1024]{1,0:T(8,128)(2,1)S(1)}, u32[]{:S(2)}, u32[]{:S(2)}) collective-permute-start(bf16[128,1024]{1,0:T(8,128)(2,1)S(1)} %collective-permute-done.7.targets_4_), channel_id=1, source_target_pairs={{0,8},{2,10},{4,12},{6,14},{8,0},{10,2},{12,4},{14,6},{16,24},{18,... | collective-permute-start | bytes 786440 | tf_op jit(solution)/shard_map/ppermute | solution.py:325
  20.2 0.5 collective-permute-start.6
  20.7 0.6 %collective-permute-start.2 = (bf16[256,512]{1,0:T(8,128)(2,1)S(1)}, bf16[256,512]{1,0:T(8,128)(2,1)S(1)}, u32[]{:S(2)}, u32[]{:S(2)}) collective-permute-start(bf16[256,512]{1,0:T(8,128)(2,1)S(1)} %slice.20), channel_id=1, source_target_pairs={{0,4},{2,6},{4,0},{6,2},{8,12},{10,14},{12,8},{14,10},{16,20},{18,... | collective-permute-start | bytes 786440 | tf_op jit(solution)/shard_map/ppermute | solution.py:325
  21.4 0.6 %collective-permute-start.3 = (bf16[256,512]{1,0:T(8,128)(2,1)S(1)}, bf16[256,512]{1,0:T(8,128)(2,1)S(1)}, u32[]{:S(2)}, u32[]{:S(2)}) collective-permute-start(bf16[256,512]{1,0:T(8,128)(2,1)S(1)} %slice.21), channel_id=1, source_target_pairs={{0,1},{1,0},{2,3},{3,2},{4,5},{5,4},{6,7},{7,6},{8,9},{9,8},{10,11... | collective-permute-start | bytes 786440 | tf_op jit(solution)/shard_map/ppermute | solution.py:328
  21.9 4.7 %collective-permute-done.9.targets_0_ = bf16[128,1024]{1,0:T(8,128)(2,1)S(1)} collective-permute-done((bf16[128,1024]{1,0:T(8,128)(2,1)S(1)}, bf16[128,1024]{1,0:T(8,128)(2,1)S(1)}, u32[]{:S(2)}, u32[]{:S(2)}) %collective-permute-start.9) | collective-permute-done | bytes 262176 | tf_op jit(solution)/shard_map/ppermute | solution.py:325
  26.7 1.0 %copy-done = bf16[512,512]{1,0:T(8,128)(2,1)S(1)} copy-done((bf16[512,512]{1,0:T(8,128)(2,1)S(1)}, bf16[512,512]{1,0:T(8,128)(2,1)}, u32[]{:S(2)}) %copy-start) | copy-done | bytes 524312
  27.7 0.9 %copy-done.1 = bf16[128,1024]{1,0:T(8,128)(2,1)S(1)} copy-done((bf16[128,1024]{1,0:T(8,128)(2,1)S(1)}, bf16[128,1024]{1,0:T(8,128)(2,1)}, u32[]{:S(2)}) %copy-start.1) | copy-done | bytes 262168
  28.8 1.8 %shard_map.49 = (f32[768,512]{1,0:T(8,128)S(1)}, f32[8,512]{1,0:T(8,128)S(1)}, f32[768,128]{1,0:T(8,128)S(1)}, f32[4,8,512]{2,1,0:T(8,128)S(1)}, f32[4,8,768]{2,1,0:T(8,128)S(1)}) custom-call(bf16[512,512]{1,0:T(8,128)(2,1)S(1)} %get-tuple-element.22.piece_0__0_.pieces_0__0__0_, bf16[512,512]{1,0:T(8,128)(2,1)S(1)} %collective-permute-done.1.piece_1__0_.pieces_0__1__0_, ...), custom_call_target="tpu_custom_call" | custom-call | flops 805306368 | tf_op jit(solution)/shard_map/pallas_call | solution.py:274
  30.5 1.6 %shard_map.50 = (f32[768,512]{1,0:T(8,128)S(1)}, f32[8,512]{1,0:T(8,128)S(1)}, f32[4,8,512]{2,1,0:T(8,128)S(1)}, f32[4,8,768]{2,1,0:T(8,128)S(1)}) custom-call(bf16[512,512]{1,0:T(8,128)(2,1)S(1)} %collective-permute-done.piece_0__0_.pieces_1__0__0_, bf16[256,512]{1,0:T(8,128)(2,1)S(1)} %collective-permute-done.2.piece_1__0_.pieces_1__1__0_, ...), custom_call_target="tpu_custom_call" | custom-call | flops 805306368 | tf_op jit(solution)/shard_map/pallas_call | solution.py:274
  32.2 1.1 %shard_map.51 = (f32[256,1024]{1,0:T(8,128)S(1)}, f32[4,8,128]{2,1,0:T(8,128)S(1)}, f32[4,8,128]{2,1,0:T(8,128)S(1)}) custom-call(bf16[512,512]{1,0:T(8,128)(2,1)S(1)} %get-tuple-element.22.piece_0__0_.pieces_0__0__0_, bf16[512,512]{1,0:T(8,128)(2,1)S(1)} %collective-permute-done.1.piece_1__0_.pieces_0__1__0_, ...), custom_call_target="tpu_custom_call" | custom-call | flops 536870912 | tf_op jit(solution)/shard_map/pallas_call | solution.py:274
  33.3 0.6 %collective-permute-start.13 = (f32[4,8,128]{2,1,0:T(8,128)S(1)}, f32[4,8,128]{2,1,0:T(8,128)S(1)}, u32[]{:S(2)}, u32[]{:S(2)}) collective-permute-start(f32[4,8,128]{2,1,0:T(8,128)S(1)} %get-tuple-element.33.mine), channel_id=1, source_target_pairs={{0,2},{2,0},{4,6},{6,4},{8,10},{10,8},{12,14},{14,12},{16,18},{18,... | collective-permute-start | bytes 49160 | tf_op jit(solution)/shard_map/ppermute | solution.py:325
  33.9 0.5 %collective-permute-start.11 = (f32[4,8,128]{2,1,0:T(8,128)S(1)}, f32[4,8,128]{2,1,0:T(8,128)S(1)}, u32[]{:S(2)}, u32[]{:S(2)}) collective-permute-start(f32[4,8,128]{2,1,0:T(8,128)S(1)} %get-tuple-element.32.mine), channel_id=1, source_target_pairs={{0,4},{2,6},{4,0},{6,2},{8,12},{10,14},{12,8},{14,10},{16,20},{18,... | collective-permute-start | bytes 49160 | tf_op jit(solution)/shard_map/ppermute | solution.py:325
  34.4 0.3 collective-permute-done.13.arrived
  34.7 1.8 %collective-permute-start.14 = (f32[4,8,128]{2,1,0:T(8,128)S(1)}, f32[4,8,128]{2,1,0:T(8,128)S(1)}, u32[]{:S(2)}, u32[]{:S(2)}) collective-permute-start(f32[4,8,128]{2,1,0:T(8,128)S(1)} %shard_map.53.mine), channel_id=1, source_target_pairs={{0,10},{2,8},{4,14},{6,12},{8,2},{10,0},{12,6},{14,4},{16,26},{18,... | collective-permute-start | bytes 49160 | tf_op jit(solution)/shard_map/ppermute | solution.py:325
  36.5 1.1 %collective-permute-done.11.arrived = f32[4,8,128]{2,1,0:T(8,128)S(1)} collective-permute-done((f32[4,8,128]{2,1,0:T(8,128)S(1)}, f32[4,8,128]{2,1,0:T(8,128)S(1)}, u32[]{:S(2)}, u32[]{:S(2)}) %collective-permute-start.11) | collective-permute-done | bytes 16416 | tf_op jit(solution)/shard_map/ppermute | solution.py:325
  37.6 0.6 %collective-permute-start.12 = (f32[4,8,128]{2,1,0:T(8,128)S(1)}, f32[4,8,128]{2,1,0:T(8,128)S(1)}, u32[]{:S(2)}, u32[]{:S(2)}) collective-permute-start(f32[4,8,128]{2,1,0:T(8,128)S(1)} %shard_map.52.rows_0_), channel_id=1, source_target_pairs={{0,1},{1,0},{2,3},{3,2},{4,5},{5,4},{6,7},{7,6},{8,9},{9,8},{10,11... | collective-permute-start | bytes 49160 | tf_op jit(solution)/shard_map/ppermute | solution.py:328
  38.2 3.1 %collective-permute-start.15 = (f32[4,8,128]{2,1,0:T(8,128)S(1)}, f32[4,8,128]{2,1,0:T(8,128)S(1)}, u32[]{:S(2)}, u32[]{:S(2)}) collective-permute-start(f32[4,8,128]{2,1,0:T(8,128)S(1)} %shard_map.54.cols_0_), channel_id=1, source_target_pairs={{0,18},{2,16},{4,22},{6,20},{8,26},{10,24},{12,30},{14,28},{16,2},... | collective-permute-start | bytes 49160 | tf_op jit(solution)/shard_map/ppermute | solution.py:325
  41.4 1.3 %collective-permute-done.15.cols_1_ = f32[4,8,128]{2,1,0:T(8,128)S(1)} collective-permute-done((f32[4,8,128]{2,1,0:T(8,128)S(1)}, f32[4,8,128]{2,1,0:T(8,128)S(1)}, u32[]{:S(2)}, u32[]{:S(2)}) %collective-permute-start.15) | collective-permute-done | bytes 16416 | tf_op jit(solution)/shard_map/ppermute | solution.py:325
  42.7 0.8 %shard_map.55 = (f32[4,4,128]{2,1,0:T(4,128)S(1)}, f32[8,128]{1,0:T(8,128)S(1)}, f32[8,128]{1,0:T(8,128)S(1)}, f32[1024,128]{1,0:T(8,128)S(1)}) custom-call(f32[768,512]{1,0:T(8,128)S(1)} %get-tuple-element.25.early_0_, f32[256,1024]{1,0:T(8,128)S(1)} %get-tuple-element.31.late, f32[4,8,128]{2,1,0:T(8,128)S(1)} %shard_map.52.rows_0_, ...), custom_call_target="tpu_custom_call" | custom-call | tf_op jit(solution)/shard_map/pallas_call | solution.py:274
  43.5 1.0 %collective-permute-start.16 = (f32[24,128]{1,0:T(8,128)S(1)}, f32[24,128]{1,0:T(8,128)S(1)}, u32[]{:S(2)}, u32[]{:S(2)}) collective-permute-start(f32[24,128]{1,0:T(8,128)S(1)} %pad_maximum_fusion), channel_id=1, source_target_pairs={{0,4},{2,6},{4,0},{6,2},{8,12},{10,14},{12,8},{14,10},{16,20},{18,... | collective-permute-start | bytes 36872 | tf_op jit(solution)/shard_map/ppermute | solution.py:325
  44.5 0.6 %slice_bitcast_fusion.1 = f32[512]{0:T(512)} fusion(f32[8,128]{1,0:T(8,128)S(1)} %get-tuple-element.34.fwd_ref), kind=kLoop, calls=%fused_computation.4 | loop fusion | bytes 4096 | tf_op jit(solution)/shard_map/reshape | solution.py:437
  45.1 0.7 %shard_map.57.mine = f32[4,4,128]{2,1,0:T(4,128)S(1)} custom-call(f32[768,512]{1,0:T(8,128)S(1)} %get-tuple-element.37.first, f32[256,1024]{1,0:T(8,128)S(1)} %get-tuple-element.31.late, f32[8,128]{1,0:T(8,128)S(1)} %get-tuple-element.34.fwd_ref, f32[1024,128]{1,0:T(8,128)S(1)} %get-tuple-element.38.bwd_down), custom_call_target="tpu_custom_call" | custom-call | flops 4194304 | tf_op jit(solution)/shard_map/pallas_call | solution.py:274
  45.8 1.4 %collective-permute-done.16 = f32[24,128]{1,0:T(8,128)S(1)} collective-permute-done((f32[24,128]{1,0:T(8,128)S(1)}, f32[24,128]{1,0:T(8,128)S(1)}, u32[]{:S(2)}, u32[]{:S(2)}) %collective-permute-start.16) | collective-permute-done | bytes 12320 | tf_op jit(solution)/shard_map/ppermute | solution.py:325
  47.3 1.2 %collective-permute-start.17 = (f32[4,4,128]{2,1,0:T(4,128)S(1)}, f32[4,4,128]{2,1,0:T(4,128)S(1)}, u32[]{:S(2)}, u32[]{:S(2)}) collective-permute-start(f32[4,4,128]{2,1,0:T(4,128)S(1)} %shard_map.58.mine), channel_id=1, source_target_pairs={{0,1},{1,0},{2,3},{3,2},{4,5},{5,4},{6,7},{7,6},{8,9},{9,8},{10,11... | collective-permute-start | bytes 24584 | tf_op jit(solution)/shard_map/ppermute | solution.py:328
  48.5 0.6 %shard_map.56 = f32[16,128]{1,0:T(8,128)} custom-call(f32[16,128]{1,0:T(8,128)S(1)} %maximum_bitcast_fusion.known), custom_call_target="tpu_custom_call" | custom-call | tf_op jit(solution)/shard_map/pallas_call | solution.py:274
  49.1 1.9 %collective-permute-done.17.arrived = f32[4,4,128]{2,1,0:T(4,128)S(1)} collective-permute-done((f32[4,4,128]{2,1,0:T(4,128)S(1)}, f32[4,4,128]{2,1,0:T(4,128)S(1)}, u32[]{:S(2)}, u32[]{:S(2)}) %collective-permute-start.17) | collective-permute-done | bytes 8224 | tf_op jit(solution)/shard_map/ppermute | solution.py:328
  51.0 0.6 %copy.7 = f32[1,4,4,128]{3,1,2,0:T(4,128)} copy(f32[1,4,4,128]{3,2,1,0:T(4,128)S(1)} %bitcast.14) | data formatting | bytes 16384
  (28 shorter events, 0.4 us)
Async XLA Ops:
  0.6 19.6 %collective-permute-start.1 = (bf16[512,512]{1,0:T(8,128)(2,1)}, bf16[512,512]{1,0:T(8,128)(2,1)S(1)}, u32[]{:S(2)}, u32[]{:S(2)}) collective-permute-start(bf16[512,512]{1,0:T(8,128)(2,1)} %source.1), channel_id=1, source_target_pairs={{0,1},{1,0},{2,3},{3,2},{4,5},{5,4},{6,7},{7,6},{8,9},{9,8},{10,11... | collective-permute-start | bytes 1572872 | tf_op jit(solution)/shard_map/ppermute | solution.py:332
  3.7 17.0 %collective-permute-start = (bf16[512,512]{1,0:T(8,128)(2,1)}, bf16[512,512]{1,0:T(8,128)(2,1)S(1)}, u32[]{:S(2)}, u32[]{:S(2)}) collective-permute-start(bf16[512,512]{1,0:T(8,128)(2,1)} %source.1), channel_id=1, source_target_pairs={{0,4},{1,5},{2,6},{3,7},{4,0},{5,1},{6,2},{7,3},{8,12},{9,13},{10,... | collective-permute-start | bytes 1572872 | tf_op jit(solution)/shard_map/ppermute | solution.py:332
  5.2 14.3 %collective-permute-start.7 = (bf16[128,1024]{1,0:T(8,128)(2,1)}, bf16[128,1024]{1,0:T(8,128)(2,1)S(1)}, u32[]{:S(2)}, u32[]{:S(2)}) collective-permute-start(bf16[128,1024]{1,0:T(8,128)(2,1)} %target.1), channel_id=1, source_target_pairs={{0,16},{2,18},{4,20},{6,22},{8,24},{10,26},{12,28},{14,30},{16,0},... | collective-permute-start | bytes 786440 | tf_op jit(solution)/shard_map/ppermute | solution.py:325
  7.8 12.4 %collective-permute-start.5 = (bf16[128,1024]{1,0:T(8,128)(2,1)}, bf16[128,1024]{1,0:T(8,128)(2,1)S(1)}, u32[]{:S(2)}, u32[]{:S(2)}) collective-permute-start(bf16[128,1024]{1,0:T(8,128)(2,1)} %target.1), channel_id=1, source_target_pairs={{0,8},{2,10},{4,12},{6,14},{8,0},{10,2},{12,4},{14,6},{16,24},{18,... | collective-permute-start | bytes 786440 | tf_op jit(solution)/shard_map/ppermute | solution.py:325
  9.3 12.0 %collective-permute-start.4 = (bf16[128,1024]{1,0:T(8,128)(2,1)}, bf16[128,1024]{1,0:T(8,128)(2,1)S(1)}, u32[]{:S(2)}, u32[]{:S(2)}) collective-permute-start(bf16[128,1024]{1,0:T(8,128)(2,1)} %target.1), channel_id=1, source_target_pairs={{0,2},{2,0},{4,6},{6,4},{8,10},{10,8},{12,14},{14,12},{16,18},{18,... | collective-permute-start | bytes 786440 | tf_op jit(solution)/shard_map/ppermute | solution.py:325
  19.5 7.2 %collective-permute-start.9 = (bf16[128,1024]{1,0:T(8,128)(2,1)S(1)}, bf16[128,1024]{1,0:T(8,128)(2,1)S(1)}, u32[]{:S(2)}, u32[]{:S(2)}) collective-permute-start(bf16[128,1024]{1,0:T(8,128)(2,1)S(1)} %collective-permute-done.7.targets_4_), channel_id=1, source_target_pairs={{0,8},{2,10},{4,12},{6,14},{8,0},{10,2},{12,4},{14,6},{16,24},{18,... | collective-permute-start | bytes 786440 | tf_op jit(solution)/shard_map/ppermute | solution.py:325
  20.2 8.6 %collective-permute-start.8 = (bf16[128,1024]{1,0:T(8,128)(2,1)S(1)}, bf16[128,1024]{1,0:T(8,128)(2,1)S(1)}, u32[]{:S(2)}, u32[]{:S(2)}) collective-permute-start(bf16[128,1024]{1,0:T(8,128)(2,1)S(1)} %collective-permute-done.7.targets_4_), channel_id=1, source_target_pairs={{0,2},{2,0},{4,6},{6,4},{8,10},{10,8},{12,14},{14,12},{16,18},{18,... | collective-permute-start | bytes 786440 | tf_op jit(solution)/shard_map/ppermute | solution.py:325
  20.2 8.6 %collective-permute-start.6 = (bf16[128,1024]{1,0:T(8,128)(2,1)S(1)}, bf16[128,1024]{1,0:T(8,128)(2,1)S(1)}, u32[]{:S(2)}, u32[]{:S(2)}) collective-permute-start(bf16[128,1024]{1,0:T(8,128)(2,1)S(1)} %collective-permute-done.5.targets_2_), channel_id=1, source_target_pairs={{0,2},{2,0},{4,6},{6,4},{8,10},{10,8},{12,14},{14,12},{16,18},{18,... | collective-permute-start | bytes 786440 | tf_op jit(solution)/shard_map/ppermute | solution.py:325
  20.7 9.8 %collective-permute-start.2 = (bf16[256,512]{1,0:T(8,128)(2,1)S(1)}, bf16[256,512]{1,0:T(8,128)(2,1)S(1)}, u32[]{:S(2)}, u32[]{:S(2)}) collective-permute-start(bf16[256,512]{1,0:T(8,128)(2,1)S(1)} %slice.20), channel_id=1, source_target_pairs={{0,4},{2,6},{4,0},{6,2},{8,12},{10,14},{12,8},{14,10},{16,20},{18,... | collective-permute-start | bytes 786440 | tf_op jit(solution)/shard_map/ppermute | solution.py:325
  21.4 9.2 %collective-permute-start.3 = (bf16[256,512]{1,0:T(8,128)(2,1)S(1)}, bf16[256,512]{1,0:T(8,128)(2,1)S(1)}, u32[]{:S(2)}, u32[]{:S(2)}) collective-permute-start(bf16[256,512]{1,0:T(8,128)(2,1)S(1)} %slice.21), channel_id=1, source_target_pairs={{0,1},{1,0},{2,3},{3,2},{4,5},{5,4},{6,7},{7,6},{8,9},{9,8},{10,11... | collective-permute-start | bytes 786440 | tf_op jit(solution)/shard_map/ppermute | solution.py:328
  26.7 5.5 %collective-permute-start.10 = (bf16[128,1024]{1,0:T(8,128)(2,1)S(1)}, bf16[128,1024]{1,0:T(8,128)(2,1)S(1)}, u32[]{:S(2)}, u32[]{:S(2)}) collective-permute-start(bf16[128,1024]{1,0:T(8,128)(2,1)S(1)} %collective-permute-done.9.targets_0_), channel_id=1, source_target_pairs={{0,2},{2,0},{4,6},{6,4},{8,10},{10,8},{12,14},{14,12},{16,18},{18,... | collective-permute-start | bytes 786440 | tf_op jit(solution)/shard_map/ppermute | solution.py:325
  26.7 1.0 %copy-start = (bf16[512,512]{1,0:T(8,128)(2,1)S(1)}, bf16[512,512]{1,0:T(8,128)(2,1)}, u32[]{:S(2)}) copy-start(bf16[512,512]{1,0:T(8,128)(2,1)} %source.1) | copy-start | bytes 1572868
  27.7 0.9 %copy-start.1 = (bf16[128,1024]{1,0:T(8,128)(2,1)S(1)}, bf16[128,1024]{1,0:T(8,128)(2,1)}, u32[]{:S(2)}) copy-start(bf16[128,1024]{1,0:T(8,128)(2,1)} %target.1) | copy-start | bytes 786436
  33.3 1.4 %collective-permute-start.13 = (f32[4,8,128]{2,1,0:T(8,128)S(1)}, f32[4,8,128]{2,1,0:T(8,128)S(1)}, u32[]{:S(2)}, u32[]{:S(2)}) collective-permute-start(f32[4,8,128]{2,1,0:T(8,128)S(1)} %get-tuple-element.33.mine), channel_id=1, source_target_pairs={{0,2},{2,0},{4,6},{6,4},{8,10},{10,8},{12,14},{14,12},{16,18},{18,... | collective-permute-start | bytes 49160 | tf_op jit(solution)/shard_map/ppermute | solution.py:325
  33.9 3.7 %collective-permute-start.11 = (f32[4,8,128]{2,1,0:T(8,128)S(1)}, f32[4,8,128]{2,1,0:T(8,128)S(1)}, u32[]{:S(2)}, u32[]{:S(2)}) collective-permute-start(f32[4,8,128]{2,1,0:T(8,128)S(1)} %get-tuple-element.32.mine), channel_id=1, source_target_pairs={{0,4},{2,6},{4,0},{6,2},{8,12},{10,14},{12,8},{14,10},{16,20},{18,... | collective-permute-start | bytes 49160 | tf_op jit(solution)/shard_map/ppermute | solution.py:325
  34.7 3.5 %collective-permute-start.14 = (f32[4,8,128]{2,1,0:T(8,128)S(1)}, f32[4,8,128]{2,1,0:T(8,128)S(1)}, u32[]{:S(2)}, u32[]{:S(2)}) collective-permute-start(f32[4,8,128]{2,1,0:T(8,128)S(1)} %shard_map.53.mine), channel_id=1, source_target_pairs={{0,10},{2,8},{4,14},{6,12},{8,2},{10,0},{12,6},{14,4},{16,26},{18,... | collective-permute-start | bytes 49160 | tf_op jit(solution)/shard_map/ppermute | solution.py:325
  37.6 3.8 %collective-permute-start.12 = (f32[4,8,128]{2,1,0:T(8,128)S(1)}, f32[4,8,128]{2,1,0:T(8,128)S(1)}, u32[]{:S(2)}, u32[]{:S(2)}) collective-permute-start(f32[4,8,128]{2,1,0:T(8,128)S(1)} %shard_map.52.rows_0_), channel_id=1, source_target_pairs={{0,1},{1,0},{2,3},{3,2},{4,5},{5,4},{6,7},{7,6},{8,9},{9,8},{10,11... | collective-permute-start | bytes 49160 | tf_op jit(solution)/shard_map/ppermute | solution.py:328
  38.2 4.5 %collective-permute-start.15 = (f32[4,8,128]{2,1,0:T(8,128)S(1)}, f32[4,8,128]{2,1,0:T(8,128)S(1)}, u32[]{:S(2)}, u32[]{:S(2)}) collective-permute-start(f32[4,8,128]{2,1,0:T(8,128)S(1)} %shard_map.54.cols_0_), channel_id=1, source_target_pairs={{0,18},{2,16},{4,22},{6,20},{8,26},{10,24},{12,30},{14,28},{16,2},... | collective-permute-start | bytes 49160 | tf_op jit(solution)/shard_map/ppermute | solution.py:325
  43.5 3.8 %collective-permute-start.16 = (f32[24,128]{1,0:T(8,128)S(1)}, f32[24,128]{1,0:T(8,128)S(1)}, u32[]{:S(2)}, u32[]{:S(2)}) collective-permute-start(f32[24,128]{1,0:T(8,128)S(1)} %pad_maximum_fusion), channel_id=1, source_target_pairs={{0,4},{2,6},{4,0},{6,2},{8,12},{10,14},{12,8},{14,10},{16,20},{18,... | collective-permute-start | bytes 36872 | tf_op jit(solution)/shard_map/ppermute | solution.py:325
  47.3 3.7 %collective-permute-start.17 = (f32[4,4,128]{2,1,0:T(4,128)S(1)}, f32[4,4,128]{2,1,0:T(4,128)S(1)}, u32[]{:S(2)}, u32[]{:S(2)}) collective-permute-start(f32[4,4,128]{2,1,0:T(4,128)S(1)} %shard_map.58.mine), channel_id=1, source_target_pairs={{0,1},{1,0},{2,3},{3,2},{4,5},{5,4},{6,7},{7,6},{8,9},{9,8},{10,11... | collective-permute-start | bytes 24584 | tf_op jit(solution)/shard_map/ppermute | solution.py:328
